TPU v7x, 32 devices: a whole 2x2x4 slice. The times are simulated.
32 devices in a mesh: dp: 4 (over y, x), expert: 8 (over z, core).
Axes of the slice: x: 2, y: 2, z: 4, core: 2. Of those that a mesh axis runs over, the one named last changes fastest.
Arguments:
- saved_input: bfloat16 [1024, 2048], P(('dp', 'expert')), may hold values from -6 to 6
- output_grad: bfloat16 [1024, 2048], P(('dp', 'expert')), may hold values from -6 to 6
- route_probs: float32 [1024, 8], P(('dp', 'expert')), may hold values from 0.02 to 0.4
- expert_choice: int32 [1024, 8], P(('dp', 'expert')), may hold values from 0 to 15, all different within a row; in each aligned block of 32 rows (0 to 31, 32 to 63, ...) at most 24 rows name the same one
- slot_expert: int32 [4, 8], replicated, may hold values from 0 to 15, as said below
- frozen_gate: bfloat16 [32, 2048, 768], P(('dp', 'expert')), as said below
- frozen_up: bfloat16 [32, 2048, 768], P(('dp', 'expert')), as said below
- frozen_down: bfloat16 [32, 768, 2048], P(('dp', 'expert')), as said below
- adapter_in: float32 [16, 64, 768], P('expert', 'dp'), may hold values from -0.21875 to 0.21875
- adapter_out: float32 [16, 64, 2048], P('expert', 'dp'), may hold values from -0.125 to 0.125
- moment_in: float32 [16, 64, 768], P('expert', 'dp'), may hold values from -3 to 3
- moment_out: float32 [16, 64, 2048], P('expert', 'dp'), may hold values from -3 to 3
- second_in: float32 [16, 64, 768], P('expert', 'dp'), may hold values from 0.01 to 1
- second_out: float32 [16, 64, 2048], P('expert', 'dp'), may hold values from 0.01 to 1
Outputs:
- input_grad: bfloat16 [1024, 2048], P(('dp', 'expert'))
- step_in: float32 [16, 64, 768], P('expert', 'dp')
- step_out: float32 [16, 64, 2048], P('expert', 'dp')
- momentum_in: float32 [16, 64, 768], P('expert', 'dp')
- momentum_out: float32 [16, 64, 2048], P('expert', 'dp')
- variance_in: float32 [16, 64, 768], P('expert', 'dp')
- variance_out: float32 [16, 64, 2048], P('expert', 'dp')
- replica_in: bfloat16 [32, 64, 768], P(('dp', 'expert'))
- replica_out: bfloat16 [32, 64, 2048], P(('dp', 'expert'))
Inputs may be any that keep to these rules, and one draw needn't show every extreme that they name: `expert_choice`: among the rows of one device no expert is named more than 24 times. `slot_expert`: the slots of index j of the expert axis host only experts 2 * j to 2 * j + 1, and each of these at least once. `frozen_gate`: slots that host the same expert hold the same frozen weights. `frozen_up`: slots that host the same expert hold the same frozen weights. `frozen_down`: slots that host the same expert hold the same frozen weights.
All inputs are finite; a program needn't handle non-finite values.
Results may differ from a plain program's by a relative error of at most 0.012.
Values may be sent and summed in bfloat16 or wider, within the bound.
No kernel may reach another device: no remote copies, remote signals or barrier semaphores. Data moves between devices by JAX's collectives and lax.ppermute only.
A program may use at most 128 MiB of HBM per device.

v0:
```python
import jax
import jax.numpy as jnp
from jax import lax
from jax.sharding import PartitionSpec as P

STEP = 100


adapter_scale_factor = 2.0
beta_one = 0.9
beta_two = 0.999
decay_rate = 0.01
adam_eps = 1e-08


def contract_product(left, right, left_dim, right_dim):
    return lax.dot_general(
        left, right, (((left_dim,), (right_dim,)), ((), ())), preferred_element_type=jnp.float32
    )


def route_rows(choice_flat, slot_expert, source, local_experts):
    column = choice_flat // local_experts
    hosted = (jnp.take(slot_expert, column, axis=1) == choice_flat[None, :]).astype(jnp.int32)
    counts = jnp.sum(hosted, axis=0)
    picked = source % counts
    running = jnp.cumsum(hosted, axis=0) - 1
    chosen = hosted * (running == picked[None, :]).astype(jnp.int32)
    dp_ids = jnp.arange(hosted.shape[0], dtype=jnp.int32)
    dest_row = jnp.sum(chosen * dp_ids[:, None], axis=0)
    row_ids = jnp.arange(choice_flat.shape[0], dtype=jnp.int32)
    earlier = (choice_flat[None, :] == choice_flat[:, None]) & (row_ids[None, :] < row_ids[:, None])
    rank = jnp.sum(earlier.astype(jnp.int32), axis=1)
    return (dest_row, column, rank)


def pack_rows(saved_input, scaled, position, buffer_size, top_count, shape_out):
    row_count = scaled.shape[0]
    row_ids = jnp.arange(row_count, dtype=jnp.int32)
    filler = jnp.full((buffer_size,), row_count, jnp.int32).at[position].set(row_ids)
    send_input = jnp.take(saved_input, filler // top_count, axis=0, mode="fill", fill_value=0)
    send_grad = jnp.take(scaled, filler, axis=0, mode="fill", fill_value=0)
    return (send_input.reshape(shape_out), send_grad.reshape(shape_out))


def adamw(param, grad, first, second):
    first_new = beta_one * first + (1.0 - beta_one) * grad
    second_new = beta_two * second + (1.0 - beta_two) * grad * grad
    corr_one = 1.0 - beta_one**STEP
    corr_two = 1.0 - beta_two**STEP
    step_dir = (
        first_new / corr_one / (jnp.sqrt(second_new / corr_two) + adam_eps) + decay_rate * param
    )
    return (step_dir, first_new, second_new)


def per_device(
    saved_input,
    output_grad,
    route_probs,
    expert_choice,
    slot_expert,
    frozen_gate,
    frozen_up,
    frozen_down,
    adapter_in,
    adapter_out,
    moment_in,
    moment_out,
    second_in,
    second_out,
):
    dp_count = lax.axis_size("dp")
    expert_count = lax.axis_size("expert")
    dp_index = lax.axis_index("dp")
    column_index = lax.axis_index("expert")
    local_experts = adapter_in.shape[0]
    token_count, top_count = expert_choice.shape
    width = saved_input.shape[1]
    row_count = token_count * top_count
    capacity = max(2, -(-3 * row_count // (2 * local_experts * expert_count)))
    buffer_size = dp_count * expert_count * capacity
    source = dp_index * expert_count + column_index
    choice_flat = expert_choice.reshape(row_count)
    dest_row, column, rank = route_rows(choice_flat, slot_expert, source, local_experts)
    scaled = (
        (route_probs[:, :, None] * output_grad[:, None, :].astype(jnp.float32))
        .astype(jnp.bfloat16)
        .reshape(row_count, width)
    )
    col_size = local_experts * expert_count * capacity
    col_position = (choice_flat % local_experts * expert_count + column) * capacity + rank
    col_shape = (local_experts, expert_count, capacity, width)
    col_input, col_grad = pack_rows(
        saved_input, scaled, col_position, col_size, top_count, col_shape
    )
    got_input, got_grad = (
        lax.all_to_all(col_input, "expert", split_axis=1, concat_axis=1, tiled=True),
        lax.all_to_all(col_grad, "expert", split_axis=1, concat_axis=1, tiled=True),
    )
    column_hosts = lax.dynamic_index_in_dim(slot_expert, column_index, 1, keepdims=False)
    dp_ids = jnp.arange(dp_count, dtype=jnp.int32)
    same_host = (column_hosts[:, None] == column_hosts[None, :]).astype(jnp.int32)
    host_count = jnp.sum(same_host, axis=1)
    host_place = jnp.sum(same_host * (dp_ids[None, :] < dp_ids[:, None]).astype(jnp.int32), axis=1)
    sources = dp_index * expert_count + jnp.arange(expert_count, dtype=jnp.int32)
    serves = sources[None, :] % host_count[:, None] == host_place[:, None]
    local_of = column_hosts - local_experts * column_index
    kept_mask = serves[:, :, None, None]
    zero_value = jnp.zeros((), jnp.bfloat16)
    picked_input = jnp.where(kept_mask, jnp.take(got_input, local_of, axis=0), zero_value)
    picked_grad = jnp.where(kept_mask, jnp.take(got_grad, local_of, axis=0), zero_value)
    arrived_input, arrived_grad = (
        lax.all_to_all(picked_input, "dp", split_axis=0, concat_axis=0, tiled=True),
        lax.all_to_all(picked_grad, "dp", split_axis=0, concat_axis=0, tiled=True),
    )
    fetched_in, fetched_out = (
        lax.all_gather(adapter_in.astype(jnp.bfloat16), "dp", axis=1, tiled=True),
        lax.all_gather(adapter_out.astype(jnp.bfloat16), "dp", axis=1, tiled=True),
    )
    hosted_local = slot_expert[dp_index, column_index] - local_experts * column_index
    owned_input = lax.dynamic_index_in_dim(fetched_in, hosted_local, 0, keepdims=False)
    own_out = lax.dynamic_index_in_dim(fetched_out, hosted_local, 0, keepdims=False)
    buffer_rows = arrived_input.reshape(buffer_size, width)
    gradient_row_block = arrived_grad.reshape(buffer_size, width)
    gate_weight = frozen_gate[0]
    up_weight = frozen_up[0]
    down_weight = frozen_down[0]
    gate_pre = jnp.dot(buffer_rows, gate_weight, preferred_element_type=jnp.float32)
    up_pre = jnp.dot(buffer_rows, up_weight, preferred_element_type=jnp.float32)
    sigmoid_gate = jax.nn.sigmoid(gate_pre)
    hidden_state = (gate_pre * sigmoid_gate * up_pre).astype(jnp.bfloat16)
    low_rank_input = contract_product(hidden_state, owned_input, 1, 1).astype(jnp.bfloat16)
    low_rank_gradient = contract_product(gradient_row_block, own_out, 1, 1).astype(jnp.bfloat16)
    hidden_gradient = contract_product(gradient_row_block, down_weight, 1, 1)
    hidden_gradient = hidden_gradient + adapter_scale_factor * jnp.dot(
        low_rank_gradient, owned_input, preferred_element_type=jnp.float32
    )
    up_grad = (hidden_gradient * gate_pre * sigmoid_gate).astype(jnp.bfloat16)
    gate_grad = (
        hidden_gradient * up_pre * sigmoid_gate * (1.0 + gate_pre * (1.0 - sigmoid_gate))
    ).astype(jnp.bfloat16)
    back_rows = (
        contract_product(gate_grad, gate_weight, 1, 1) + contract_product(up_grad, up_weight, 1, 1)
    ).astype(jnp.bfloat16)
    incoming_gradient = adapter_scale_factor * contract_product(
        low_rank_gradient, hidden_state, 0, 0
    )
    outgoing_gradient = adapter_scale_factor * contract_product(
        low_rank_input, gradient_row_block, 0, 0
    )
    back_block = back_rows.reshape(dp_count, expert_count, capacity, width)
    came_back = lax.all_to_all(back_block, "dp", split_axis=0, concat_axis=0, tiled=True)
    pieces_back = []
    for which_local in range(local_experts):
        chosen_mask = (serves & (local_of == which_local)[:, None])[:, :, None, None]
        pieces_back.append(jnp.sum(jnp.where(chosen_mask, came_back, zero_value), axis=0))
    gone_back = lax.all_to_all(
        jnp.stack(pieces_back), "expert", split_axis=1, concat_axis=1, tiled=True
    )
    per_row = jnp.take(gone_back.reshape(col_size, width), col_position, axis=0)
    input_grad = jnp.sum(
        per_row.reshape(token_count, top_count, width).astype(jnp.float32), axis=1
    ).astype(jnp.bfloat16)
    selector = (jnp.arange(local_experts, dtype=jnp.int32) == hosted_local).astype(jnp.float32)
    placed_in = selector[:, None, None] * incoming_gradient[None, :, :]
    placed_out = selector[:, None, None] * outgoing_gradient[None, :, :]
    summed_in, summed_out = (
        lax.psum_scatter(placed_in, "dp", scatter_dimension=1, tiled=True),
        lax.psum_scatter(placed_out, "dp", scatter_dimension=1, tiled=True),
    )
    step_in, momentum_in, variance_in = adamw(adapter_in, summed_in, moment_in, second_in)
    step_out, momentum_out, variance_out = adamw(adapter_out, summed_out, moment_out, second_out)
    copied_in, copied_out = (
        lax.all_gather(step_in.astype(jnp.bfloat16), "dp", axis=1, tiled=True),
        lax.all_gather(step_out.astype(jnp.bfloat16), "dp", axis=1, tiled=True),
    )
    replica_in = lax.dynamic_index_in_dim(copied_in, hosted_local, 0, keepdims=True)
    replica_out = lax.dynamic_index_in_dim(copied_out, hosted_local, 0, keepdims=True)
    return (
        input_grad,
        step_in,
        step_out,
        momentum_in,
        momentum_out,
        variance_in,
        variance_out,
        replica_in,
        replica_out,
    )


def solution(mesh):
    return jax.shard_map(
        per_device,
        mesh=mesh,
        in_specs=(
            P(("dp", "expert"), None),
            P(("dp", "expert"), None),
            P(("dp", "expert"), None),
            P(("dp", "expert"), None),
            P(),
            P(("dp", "expert"), None, None),
            P(("dp", "expert"), None, None),
            P(("dp", "expert"), None, None),
            P("expert", "dp", None),
            P("expert", "dp", None),
            P("expert", "dp", None),
            P("expert", "dp", None),
            P("expert", "dp", None),
            P("expert", "dp", None),
        ),
        out_specs=(
            P(("dp", "expert"), None),
            P("expert", "dp", None),
            P("expert", "dp", None),
            P("expert", "dp", None),
            P("expert", "dp", None),
            P("expert", "dp", None),
            P("expert", "dp", None),
            P(("dp", "expert"), None, None),
            P(("dp", "expert"), None, None),
        ),
        check_vma=False,
    )
```

profile of v0, /device:TPU:0, one launch (start us, length us, event | category | flops | bytes accessed | tf_op | source)
XLA Modules:
  0.0 375.1 jit_solution(5800526938693478548)
XLA Ops:
  10.6 6.0 %gather_fusion.1 = bf16[384,2048]{1,0:T(8,128)(2,1)} fusion(bf16[32,2048]{1,0:T(8,128)(2,1)} %param.16, s32[1024]{0:T(1024)S(1)} %pad_clamp_fusion.1), kind=kCustom, calls=%fused_computation.3 | custom fusion | bytes 3147264 | tf_op jit(solution)/shard_map/jit(_take)/gather | solution.py:41
  16.6 2.8 copy_select_fusion
  19.4 6.5 %all-to-all-start.2 = ((bf16[2,8,24,2048]{3,2,0,1:T(8,128)(2,1)}), bf16[2,8,24,2048]{3,2,0,1:T(8,128)(2,1)}, u32[]{:S(2)}, u32[]{:S(2)}) async-start(bf16[2,8,24,2048]{3,2,0,1:T(8,128)(2,1)} %copy_select_fusion), calls=%async_computation.2 | async-start | bytes 3145728 | tf_op jit(solution)/shard_map/all_to_all | solution.py:98
  29.3 6.4 %gather_fusion = bf16[384,2048]{1,0:T(8,128)(2,1)} fusion(bf16[256,2048]{1,0:T(8,128)(2,1)} %fusion.9, s32[1024]{0:T(1024)S(1)} %pad_clamp_fusion.3), kind=kCustom, calls=%fused_computation.2 | custom fusion | bytes 3147264 | tf_op jit(solution)/shard_map/jit(_take)/gather | solution.py:42
  35.8 2.8 copy_select_fusion.1
  38.5 25.2 %all-to-all-done.2 = bf16[2,8,24,2048]{3,2,0,1:T(8,128)(2,1)} async-done(((bf16[2,8,24,2048]{3,2,0,1:T(8,128)(2,1)}), bf16[2,8,24,2048]{3,2,0,1:T(8,128)(2,1)}, u32[]{:S(2)}, u32[]{:S(2)}) %all-to-all-start.2) | async-done | bytes 1572896 | tf_op jit(solution)/shard_map/all_to_all | solution.py:98
  63.8 4.3 %all-to-all-start = ((bf16[2,8,24,2048]{3,2,0,1:T(8,128)(2,1)}), bf16[2,8,24,2048]{3,2,0,1:T(8,128)(2,1)}, u32[]{:S(2)}, u32[]{:S(2)}) async-start(bf16[2,8,24,2048]{3,2,0,1:T(8,128)(2,1)} %copy_select_fusion.1), calls=%async_computation | async-start | bytes 3145728 | tf_op jit(solution)/shard_map/all_to_all | solution.py:99
  69.9 3.8 %gather_fusion.4 = bf16[4,8,24,2048]{3,2,1,0:T(8,128)(2,1)} fusion(bf16[2,8,24,2048]{3,2,0,1:T(8,128)(2,1)} %all-to-all-done.2, s32[1024]{0:T(1024)S(1)} %pad_clamp_fusion.2), kind=kCustom, calls=%fused_computation.1.clone | custom fusion | bytes 6291472 | tf_op jit(solution)/shard_map/jit(_take)/gather | solution.py:111
  73.7 32.2 %all-to-all-done = bf16[2,8,24,2048]{3,2,0,1:T(8,128)(2,1)} async-done(((bf16[2,8,24,2048]{3,2,0,1:T(8,128)(2,1)}), bf16[2,8,24,2048]{3,2,0,1:T(8,128)(2,1)}, u32[]{:S(2)}, u32[]{:S(2)}) %all-to-all-start) | async-done | bytes 1572896 | tf_op jit(solution)/shard_map/all_to_all | solution.py:99
  105.9 3.9 %gather_fusion.3 = bf16[4,8,24,2048]{3,2,1,0:T(8,128)(2,1)} fusion(bf16[2,8,24,2048]{3,2,0,1:T(8,128)(2,1)} %all-to-all-done, s32[1024]{0:T(1024)S(1)} %pad_clamp_fusion.2), kind=kCustom, calls=%fused_computation.clone | custom fusion | bytes 6291472 | tf_op jit(solution)/shard_map/jit(_take)/gather | solution.py:112
  109.7 5.3 %select_select_fusion.1 = (bf16[4,8,24,2048]{3,2,1,0:T(8,128)(2,1)}, bf16[4,8,24,2048]{3,2,1,0:T(8,128)(2,1)S(1)}) fusion(bf16[4,8,24,2048]{3,2,1,0:T(8,128)(2,1)} %gather_fusion.3, pred[4]{0:T(512)(128)(4,1)S(1)} %get-tuple-element.26, pred[4,8]{1,0:T(4,128)(4,1)S(1)} %get-tuple-element.25, bf16[4,8,24,2048]{3,2,1,0:T(8,128)(2,1)} %gather_fusion.4), kind=kLoop, calls=%fused_computation.17 | loop fusion | flops 6291456 | bytes 12582948 | tf_op jit(solution)/shard_map/jit(_where)/select_n | solution.py:112
  115.0 39.9 %all_to_all.30 = bf16[4,8,24,2048]{3,2,1,0:T(8,128)(2,1)} all-to-all(bf16[4,8,24,2048]{3,2,1,0:T(8,128)(2,1)S(1)} %get-tuple-element.33), channel_id=1, replica_groups=mesh['dp'=4,'expert'=8] {'dp'}, dimensions={0} | all-to-all | bytes 6291456 | tf_op jit(solution)/shard_map/all_to_all | solution.py:114
  155.0 4.8 %all-to-all-start.1 = ((bf16[4,8,24,2048]{3,2,1,0:T(8,128)(2,1)}), bf16[4,8,24,2048]{3,2,1,0:T(8,128)(2,1)}, u32[]{:S(2)}, u32[]{:S(2)}) async-start(bf16[4,8,24,2048]{3,2,1,0:T(8,128)(2,1)} %get-tuple-element.32), calls=%async_computation.1 | async-start | bytes 6291456 | tf_op jit(solution)/shard_map/all_to_all | solution.py:115
  161.1 37.8 %all_gather.13 = bf16[2,64,768]{2,1,0:T(8,128)(2,1)S(1)} all-gather(bf16[2,16,768]{2,1,0:T(8,128)(2,1)S(1)} %convert_element_type.64), channel_id=1, replica_groups=mesh['dp'=4,'expert'=8] {'dp'}, dimensions={1}, use_global_device_ids=true | all-gather | bytes 245760 | tf_op jit(solution)/shard_map/all_gather | solution.py:118
  199.0 5.6 %fusion.2 = f32[768,768]{1,0:T(8,128)S(1)} fusion(bf16[768,2048]{1,0:T(8,128)(2,1)} %bitcast.55, bf16[1,2048,768]{2,1,0:T(8,128)(2,1)} %param.21), kind=kOutput, calls=%fused_computation.9 | convolution fusion | flops 2415919104 | bytes 8650752 | tf_op jit(solution)/shard_map/dot_general | solution.py:129
  206.0 4.5 %multiply_convert_fusion = (bf16[768,768]{1,0:T(8,128)(2,1)}, f32[768,768]{1,0:T(8,128)}) fusion(f32[768,768]{1,0:T(8,128)S(1)} %fusion.2, bf16[768,2048]{1,0:T(8,128)(2,1)S(1)} %bitcast.56, bf16[1,2048,768]{2,1,0:T(8,128)(2,1)S(1)} %copy-done), kind=kOutput, calls=%fused_computation.20 | convolution fusion | flops 2419458048 | bytes 12189696 | tf_op jit(solution)/shard_map/dot_general | solution.py:130
  210.5 4.3 %convolution_multiply_fusion = f32[64,2048]{1,0:T(8,128)} fusion(bf16[768,2048]{1,0:T(8,128)(2,1)} %bitcast.4, bf16[768,768]{1,0:T(8,128)(2,1)} %get-tuple-element.34, bf16[2,64,768]{2,1,0:T(8,128)(2,1)S(1)} %all_gather.13, s32[]{:T(128)S(6)} %select_n.159), kind=kOutput, calls=%fused_computation.25 | convolution fusion | flops 277004288 | bytes 4947972 | tf_op jit(solution)/shard_map/dot_general | solution.py:17
  217.0 6.9 %fusion.7 = f32[768,768]{1,0:T(8,128)} fusion(bf16[768,2048]{1,0:T(8,128)(2,1)} %bitcast.4, bf16[1,768,2048]{2,1,0:T(8,128)(2,1)} %param.23), kind=kOutput, calls=%fused_computation.14 | convolution fusion | flops 2415919104 | bytes 8650752 | tf_op jit(solution)/shard_map/dot_general | solution.py:17
  223.9 20.0 %reduce-scatter.5.cloned.1.call-done = f32[2,16,2048]{2,1,0:T(8,128)} async-done(((f32[2,64,2048]{2,1,0:T(8,128)}), f32[2,16,2048]{2,1,0:T(8,128)}) %reduce-scatter.5.cloned.1.call-update) | async-done | bytes 262160 | tf_op jit(solution)/shard_map/reduce_scatter | solution.py:170
  246.2 10.3 %all_gather.12 = bf16[2,64,2048]{2,1,0:T(8,128)(2,1)S(1)} all-gather(bf16[2,16,2048]{2,1,0:T(8,128)(2,1)S(1)} %get-tuple-element.30), channel_id=1, replica_groups=mesh['dp'=4,'expert'=8] {'dp'}, dimensions={1}, use_global_device_ids=true | all-gather | bytes 655360 | tf_op jit(solution)/shard_map/all_gather | solution.py:119
  256.5 3.1 convolution_convert_fusion.1
  261.7 3.3 fusion
  265.0 4.2 %add_convert_fusion = bf16[768,2048]{1,0:T(8,128)(2,1)} fusion(f32[768,2048]{1,0:T(8,128)S(1)} %fusion, bf16[1,2048,768]{2,1,0:T(8,128)(2,1)S(1)} %copy-done, f32[768,768]{1,0:T(8,128)S(1)} %multiply_add_fusion, f32[768,768]{1,0:T(8,128)S(1)} %copy-done.21), kind=kOutput, calls=%fused_computation.6 | convolution fusion | flops 2422603776 | bytes 17301504 | tf_op jit(solution)/shard_map/dot_general | solution.py:17
  269.2 4.8 %all-to-all-start.4 = ((bf16[4,8,24,2048]{3,2,1,0:T(8,128)(2,1)}), bf16[4,8,24,2048]{3,2,1,0:T(8,128)(2,1)}, u32[]{:S(2)}, u32[]{:S(2)}) async-start(bf16[4,8,24,2048]{3,2,1,0:T(8,128)(2,1)} %bitcast.57), calls=%async_computation.4 | async-start | bytes 6291456 | tf_op jit(solution)/shard_map/all_to_all | solution.py:153
  274.1 34.1 %all-to-all-done.4 = bf16[4,8,24,2048]{3,2,1,0:T(8,128)(2,1)} async-done(((bf16[4,8,24,2048]{3,2,1,0:T(8,128)(2,1)}), bf16[4,8,24,2048]{3,2,1,0:T(8,128)(2,1)}, u32[]{:S(2)}, u32[]{:S(2)}) %all-to-all-start.4) | async-done | bytes 3145760 | tf_op jit(solution)/shard_map/all_to_all | solution.py:153
  308.2 3.7 select_reduce_fusion.1
  313.3 4.8 %all-to-all-start.5 = ((bf16[2,8,24,2048]{3,2,0,1:T(8,128)(2,1)}), bf16[2,8,24,2048]{3,2,0,1:T(8,128)(2,1)}, u32[]{:S(2)}, u32[]{:S(2)}) async-start(bf16[2,8,24,2048]{3,2,0,1:T(8,128)(2,1)} %pad_maximum_fusion), calls=%async_computation.5 | async-start | bytes 3145728 | tf_op jit(solution)/shard_map/all_to_all | solution.py:158
  320.7 11.7 %all_gather.15 = bf16[2,64,2048]{2,1,0:T(8,128)(2,1)S(1)} all-gather(bf16[2,16,2048]{2,1,0:T(8,128)(2,1)S(1)} %copy-done.3), channel_id=1, replica_groups=mesh['dp'=4,'expert'=8] {'dp'}, dimensions={1}, use_global_device_ids=true | all-gather | bytes 655360 | tf_op jit(solution)/shard_map/all_gather | solution.py:176
  333.1 13.8 %reduce-scatter.3.cloned.1.call-done = f32[2,16,768]{2,1,0:T(8,128)} async-done(((f32[2,64,768]{2,1,0:T(8,128)}), f32[2,16,768]{2,1,0:T(8,128)}) %reduce-scatter.3.cloned.1.call-update) | async-done | bytes 98320 | tf_op jit(solution)/shard_map/reduce_scatter | solution.py:169
  348.6 8.9 %all_gather.14 = bf16[2,64,768]{2,1,0:T(8,128)(2,1)S(1)} all-gather(bf16[2,16,768]{2,1,0:T(8,128)(2,1)S(1)} %get-tuple-element.20), channel_id=1, replica_groups=mesh['dp'=4,'expert'=8] {'dp'}, dimensions={1}, use_global_device_ids=true | all-gather | bytes 245760 | tf_op jit(solution)/shard_map/all_gather | solution.py:175
  358.2 2.7 copy.64
  360.9 5.0 %gather_fusion.2 = bf16[256,2048]{1,0:T(8,128)(2,1)} fusion(bf16[384,2048]{1,0:T(8,128)(2,1)} %bitcast.52, s32[1024]{0:T(1024)S(1)} %pad_clamp_fusion), kind=kCustom, calls=%fused_computation.4 | custom fusion | bytes 2098176 | tf_op jit(solution)/shard_map/jit(_take)/gather | solution.py:161
  (97 shorter events, 26.9 us)
Async XLA Ops:
  7.2 198.8 %copy-start = (bf16[1,2048,768]{2,1,0:T(8,128)(2,1)S(1)}, bf16[1,2048,768]{2,1,0:T(8,128)(2,1)}, u32[]{:S(2)}) copy-start(bf16[1,2048,768]{2,1,0:T(8,128)(2,1)} %param.22) | copy-start | bytes 9437188
  8.5 0.6 copy-start.9
  8.5 0.6 copy-start.11
  10.5 6.1 %copy-start.6 = (s32[384]{0:T(512)}, s32[384]{0:T(512)S(1)}, u32[]{:S(2)}) copy-start(s32[384]{0:T(512)S(1)} %scatter_custom_fusion) | copy-start | bytes 4612
  19.4 7.2 %copy-start.5 = (bf16[32,2048]{1,0:T(8,128)(2,1)S(1)}, bf16[32,2048]{1,0:T(8,128)(2,1)}, u32[]{:S(2)}) copy-start(bf16[32,2048]{1,0:T(8,128)(2,1)} %param.17) | copy-start | bytes 393220
  19.4 44.4 %all-to-all-start.2 = ((bf16[2,8,24,2048]{3,2,0,1:T(8,128)(2,1)}), bf16[2,8,24,2048]{3,2,0,1:T(8,128)(2,1)}, u32[]{:S(2)}, u32[]{:S(2)}) async-start(bf16[2,8,24,2048]{3,2,0,1:T(8,128)(2,1)} %copy_select_fusion), calls=%async_computation.2 | async-start | bytes 3145728 | tf_op jit(solution)/shard_map/all_to_all | solution.py:98
  29.3 6.4 %copy-start.7 = (pred[2,8,24]{2,0,1:T(4,128)(4,1)S(1)}, pred[2,8,24]{2,0,1:T(4,128)(4,1)}, u32[]{:S(2)}) copy-start(pred[2,8,24]{2,0,1:T(4,128)(4,1)} %copy.59) | copy-start | bytes 1156
  38.5 29.5 %copy-start.8 = (s32[4,8]{1,0:T(4,128)S(1)}, s32[4,8]{1,0:T(4,128)}, u32[]{:S(2)}) copy-start(s32[4,8]{1,0:T(4,128)} %param.20) | copy-start | bytes 388
  63.8 42.1 %all-to-all-start = ((bf16[2,8,24,2048]{3,2,0,1:T(8,128)(2,1)}), bf16[2,8,24,2048]{3,2,0,1:T(8,128)(2,1)}, u32[]{:S(2)}, u32[]{:S(2)}) async-start(bf16[2,8,24,2048]{3,2,0,1:T(8,128)(2,1)} %copy_select_fusion.1), calls=%async_computation | async-start | bytes 3145728 | tf_op jit(solution)/shard_map/all_to_all | solution.py:99
  69.9 39.8 %copy-start.14 = (pred[4,8]{1,0:T(4,128)(4,1)}, pred[4,8]{1,0:T(4,128)(4,1)S(1)}, u32[]{:S(2)}) copy-start(pred[4,8]{1,0:T(4,128)(4,1)S(1)} %get-tuple-element.25) | copy-start | bytes 100
  155.0 6.1 %copy-start.4 = (f32[2,16,768]{2,1,0:T(8,128)S(1)}, f32[2,16,768]{2,1,0:T(8,128)}, u32[]{:S(2)}) copy-start(f32[2,16,768]{2,1,0:T(8,128)} %param.24) | copy-start | bytes 294916
  155.0 55.5 %all-to-all-start.1 = ((bf16[4,8,24,2048]{3,2,1,0:T(8,128)(2,1)}), bf16[4,8,24,2048]{3,2,1,0:T(8,128)(2,1)}, u32[]{:S(2)}, u32[]{:S(2)}) async-start(bf16[4,8,24,2048]{3,2,1,0:T(8,128)(2,1)} %get-tuple-element.32), calls=%async_computation.1 | async-start | bytes 6291456 | tf_op jit(solution)/shard_map/all_to_all | solution.py:115
  159.8 84.1 %reduce-scatter.5.cloned.1.call-start = ((), (), s32[]{:S(2)}) async-start(), calls=%async_computation.9 | async-start | bytes 1310720 | tf_op jit(solution)/shard_map/reduce_scatter | solution.py:170
  199.0 15.8 %copy-start.16 = (f32[2]{0:T(128)}, f32[2]{0:T(128)S(1)}, u32[]{:S(2)}) copy-start(f32[2]{0:T(128)S(1)} %compare_convert_fusion) | copy-start | bytes 28
  199.0 7.0 %copy-start.1 = (bf16[4,8,24,2048]{3,2,1,0:T(8,128)(2,1)S(1)}, bf16[4,8,24,2048]{3,2,1,0:T(8,128)(2,1)}, u32[]{:S(2)}) copy-start(bf16[4,8,24,2048]{3,2,1,0:T(8,128)(2,1)} %all_to_all.30) | copy-start | bytes 9437188
  204.6 1.4 copy-start.20
  256.5 3.1 copy-start.2
  256.5 3.7 copy-start.21
  256.5 4.0 %copy-start.22 = (f32[768,768]{1,0:T(8,128)S(1)}, f32[768,768]{1,0:T(8,128)}, u32[]{:S(2)}) copy-start(f32[768,768]{1,0:T(8,128)} %get-tuple-element.35) | copy-start | bytes 7077892
  259.6 2.1 copy-start.19
  269.2 4.8 %copy-start.15 = (pred[4,8]{1,0:T(4,128)(4,1)S(1)}, pred[4,8]{1,0:T(4,128)(4,1)}, u32[]{:S(2)}) copy-start(pred[4,8]{1,0:T(4,128)(4,1)} %copy-done.14) | copy-start | bytes 100
  269.2 4.8 %copy-start.18 = (pred[4]{0:T(512)(128)(4,1)S(1)}, pred[4]{0:T(512)(128)(4,1)}, u32[]{:S(2)}) copy-start(pred[4]{0:T(512)(128)(4,1)} %get-tuple-element.12) | copy-start | bytes 16
  269.2 39.0 %copy-start.13 = (pred[4,8]{1,0:T(4,128)(4,1)S(1)}, pred[4,8]{1,0:T(4,128)(4,1)}, u32[]{:S(2)}) copy-start(pred[4,8]{1,0:T(4,128)(4,1)} %get-tuple-element.24) | copy-start | bytes 100
  269.2 39.0 %all-to-all-start.4 = ((bf16[4,8,24,2048]{3,2,1,0:T(8,128)(2,1)}), bf16[4,8,24,2048]{3,2,1,0:T(8,128)(2,1)}, u32[]{:S(2)}, u32[]{:S(2)}) async-start(bf16[4,8,24,2048]{3,2,1,0:T(8,128)(2,1)} %bitcast.57), calls=%async_computation.4 | async-start | bytes 6291456 | tf_op jit(solution)/shard_map/all_to_all | solution.py:153
  313.2 6.4 %copy-start.17 = (f32[2]{0:T(128)S(1)}, f32[2]{0:T(128)}, u32[]{:S(2)}) copy-start(f32[2]{0:T(128)} %copy-done.16) | copy-start | bytes 28
  313.2 7.3 %copy-start.10 = (s32[256]{0:T(256)S(1)}, s32[256]{0:T(256)}, u32[]{:S(2)}) copy-start(s32[256]{0:T(256)} %copy-done.9) | copy-start | bytes 3076
  313.2 7.4 %copy-start.12 = (s32[256,1]{0,1:T(1,128)S(1)}, s32[256,1]{0,1:T(1,128)}, u32[]{:S(2)}) copy-start(s32[256,1]{0,1:T(1,128)} %copy-done.11) | copy-start | bytes 3076
  313.2 7.5 %copy-start.3 = (bf16[2,16,2048]{2,1,0:T(8,128)(2,1)S(1)}, bf16[2,16,2048]{2,1,0:T(8,128)(2,1)}, u32[]{:S(2)}) copy-start(bf16[2,16,2048]{2,1,0:T(8,128)(2,1)} %get-tuple-element.16) | copy-start | bytes 393220
  313.3 44.9 %all-to-all-start.5 = ((bf16[2,8,24,2048]{3,2,0,1:T(8,128)(2,1)}), bf16[2,8,24,2048]{3,2,0,1:T(8,128)(2,1)}, u32[]{:S(2)}, u32[]{:S(2)}) async-start(bf16[2,8,24,2048]{3,2,0,1:T(8,128)(2,1)} %pad_maximum_fusion), calls=%async_computation.5 | async-start | bytes 3145728 | tf_op jit(solution)/shard_map/all_to_all | solution.py:158
  318.0 28.8 %reduce-scatter.3.cloned.1.call-start = ((), (), s32[]{:S(2)}) async-start(), calls=%async_computation.8 | async-start | bytes 491520 | tf_op jit(solution)/shard_map/reduce_scatter | solution.py:169
Sparse Core Ops, SparseCore 0:
  217.1 26.6 reduce-scatter.4
  321.6 25.1 reduce-scatter.2
where the time goes:
time: 376 us; the launch traced here: 375 us
  waiting for transfers between devices  125 us (33%)
  blocking collectives  109 us (29%)
  local copies, waits for them, and re-layouts  37.7 us (10%)
  matrix products  33.9 us (9%)
  other arithmetic  29.3 us (8%)
  starting transfers between devices  25.2 us (7%)
  between operations  15.1 us (4%)
    all_to_all x1, blocking collectives, per_device(): lax.all_to_all(picked_input, 'dp', split_axis=0, concat_axis=0, tiled=True)  39.9 us
    all_gather x1, blocking collectives, per_device(): lax.all_gather(adapter_in.astype(jnp.bfloat16), 'dp', axis=1, tiled=True)  37.8 us
    all_to_all x1, waiting for transfers between devices, per_device(): lax.all_to_all(back_block, 'dp', split_axis=0, concat_axis=0, tiled=True)  34.1 us
    all_to_all x1, waiting for transfers between devices, per_device(): lax.all_to_all(col_grad, 'expert', split_axis=1, concat_axis=1, tiled=True)  32.2 us
    all_to_all x1, waiting for transfers between devices, per_device(): lax.all_to_all(col_input, 'expert', split_axis=1, concat_axis=1, tiled=True)  25.2 us
    dot_general x6, matrix products, contract_product(): lax.dot_general(left, right, (((left_dim,), (right_dim,)), ((), ())), pre...  23.4 us
    reduce_scatter x1, waiting for transfers between devices, per_device(): lax.psum_scatter(placed_out, 'dp', scatter_dimension=1, tiled=True)  20 us
    reduce_scatter x1, waiting for transfers between devices, per_device(): lax.psum_scatter(placed_in, 'dp', scatter_dimension=1, tiled=True)  13.8 us
  transfers between devices with their start and end apart: 7, of which 5 were waited for; matrix products, arithmetic and copies ran while one was open for 11% of the time, Pallas kernels for 0%

commit v1 on v0

--- a/solution.py
+++ b/solution.py
@@ -54,7 +54,7 @@
     return (step_dir, first_new, second_new)
 
 
-def per_device(
+def packed_device(
     saved_input,
     output_grad,
     route_probs,
@@ -190,6 +190,244 @@
     )
 
 
+def flip_chip(array, distance, size):
+    return lax.ppermute(array, "expert", [(i, i ^ (2 * distance)) for i in range(size)])
+
+
+def flip_core(array, size):
+    return lax.ppermute(array, "expert", [(i, i ^ 1) for i in range(size)])
+
+
+def flip_plane(array, dp_count, size, masks):
+    pairs = [
+        (row * size + col, (row ^ masks[col % 2]) * size + col)
+        for row in range(dp_count)
+        for col in range(size)
+    ]
+    return lax.ppermute(array, ("dp", "expert"), pairs)
+
+
+def add_rounded(left, right):
+    return (left.astype(jnp.float32) + right.astype(jnp.float32)).astype(jnp.bfloat16)
+
+
+def dense_probs(route_probs, expert_choice, expert_total):
+    ids = jnp.arange(expert_total, dtype=jnp.int32)
+    named = expert_choice[:, :, None] == ids[None, None, :]
+    return jnp.sum(jnp.where(named, route_probs[:, :, None], 0.0), axis=1)
+
+
+def split_three(value):
+    high = lax.reduce_precision(value, 8, 7)
+    rest = value - high
+    middle = lax.reduce_precision(rest, 8, 7)
+    low = rest - middle
+    return [part.astype(jnp.bfloat16) for part in (high, middle, low)]
+
+
+def host_tables(slot_expert, dp_count, column_index, dp_index, local_experts):
+    hosts = lax.dynamic_index_in_dim(slot_expert, column_index, 1, keepdims=False)
+    local_of = hosts - local_experts * column_index
+    dp_ids = jnp.arange(dp_count, dtype=jnp.int32)
+    mine = lax.dynamic_index_in_dim(hosts, dp_index, 0, keepdims=False)
+    same = (hosts == mine).astype(jnp.int32)
+    count = jnp.sum(same)
+    place = jnp.sum(same * (dp_ids < dp_index).astype(jnp.int32))
+    return (local_of, mine, count, place)
+
+
+def pick_local(stacked, local_of):
+    count = stacked.shape[0]
+    total = jnp.zeros((local_of.shape[0],) + stacked.shape[1:], stacked.dtype)
+    for which in range(count):
+        chosen = (local_of == which).reshape((-1,) + (1,) * (stacked.ndim - 1))
+        total = jnp.where(chosen, stacked[which][None], total)
+    return total
+
+
+def expert_rows(rows, gradient, gate_weight, up_weight, down_weight, owned_input, own_out):
+    gate_pre = jnp.dot(rows, gate_weight, preferred_element_type=jnp.float32)
+    up_pre = jnp.dot(rows, up_weight, preferred_element_type=jnp.float32)
+    sigmoid_gate = jax.nn.sigmoid(gate_pre)
+    hidden_state = (gate_pre * sigmoid_gate * up_pre).astype(jnp.bfloat16)
+    low_rank_input = contract_product(hidden_state, owned_input, 1, 1).astype(jnp.bfloat16)
+    low_rank_gradient = contract_product(gradient, own_out, 1, 1).astype(jnp.bfloat16)
+    hidden_gradient = contract_product(gradient, down_weight, 1, 1)
+    hidden_gradient = hidden_gradient + adapter_scale_factor * jnp.dot(
+        low_rank_gradient, owned_input, preferred_element_type=jnp.float32
+    )
+    up_grad = (hidden_gradient * gate_pre * sigmoid_gate).astype(jnp.bfloat16)
+    gate_grad = (
+        hidden_gradient * up_pre * sigmoid_gate * (1.0 + gate_pre * (1.0 - sigmoid_gate))
+    ).astype(jnp.bfloat16)
+    back_rows = (
+        contract_product(gate_grad, gate_weight, 1, 1) + contract_product(up_grad, up_weight, 1, 1)
+    ).astype(jnp.bfloat16)
+    incoming = adapter_scale_factor * contract_product(low_rank_gradient, hidden_state, 0, 0)
+    outgoing = adapter_scale_factor * contract_product(low_rank_input, gradient, 0, 0)
+    return (back_rows, incoming, outgoing)
+
+
+def dense_device(
+    saved_input,
+    output_grad,
+    route_probs,
+    expert_choice,
+    slot_expert,
+    frozen_gate,
+    frozen_up,
+    frozen_down,
+    adapter_in,
+    adapter_out,
+    moment_in,
+    moment_out,
+    second_in,
+    second_out,
+):
+    dp_count = lax.axis_size("dp")
+    expert_count = lax.axis_size("expert")
+    dp_index = lax.axis_index("dp")
+    column_index = lax.axis_index("expert")
+    local_experts = adapter_in.shape[0]
+    tokens, top_count = expert_choice.shape
+    width = saved_input.shape[1]
+    hidden = adapter_in.shape[2]
+    expert_total = local_experts * expert_count
+    chips = expert_count // 2
+    core = column_index % 2
+    bf16 = jnp.bfloat16
+
+    parts = split_three(dense_probs(route_probs, expert_choice, expert_total))
+    spare = -(-3 * expert_total // 128) * 128 - 3 * expert_total
+    block = jnp.concatenate(
+        [saved_input, output_grad, *parts, jnp.zeros((tokens, spare), bf16)], axis=1
+    )
+    gathered = [block] + [flip_chip(block, z, expert_count) for z in range(1, chips)]
+    mine_column = jnp.concatenate(gathered, axis=0)
+
+    local_of, hosted, host_count, host_place = host_tables(
+        slot_expert, dp_count, column_index, dp_index, local_experts
+    )
+    adapters = jnp.concatenate([adapter_in, adapter_out], axis=2).astype(bf16)
+    fetched = lax.all_to_all(
+        pick_local(adapters, local_of), "dp", split_axis=0, concat_axis=0, tiled=True
+    )
+    rank = dp_count * adapter_in.shape[1]
+    fetched = fetched.reshape(rank, hidden + width)
+    owned_input = fetched[:, :hidden]
+    own_out = fetched[:, hidden:]
+
+    other_column = flip_core(mine_column, expert_count)
+    own_chunk = jnp.concatenate([mine_column, other_column], axis=0)
+    side_chunk = flip_plane(own_chunk, dp_count, expert_count, (1, 2))
+    half = chips * tokens
+    far_mine = flip_plane(side_chunk[:half], dp_count, expert_count, (2, 1))
+    cross_chunk = flip_core(side_chunk, expert_count)
+    far_other = flip_core(far_mine, expert_count)
+    arrived = jnp.concatenate([own_chunk, side_chunk, cross_chunk, far_mine, far_other], axis=0)
+
+    near, far = jnp.where(core == 0, 1, 2), jnp.where(core == 0, 2, 1)
+    chip_ids = jnp.arange(chips, dtype=jnp.int32)
+    chip_index = column_index // 2
+
+    def sources(row, col_core):
+        return row * expert_count + (chip_index ^ chip_ids) * 2 + col_core
+
+    ordered = jnp.concatenate(
+        [
+            sources(dp_index, core),
+            sources(dp_index, 1 - core),
+            sources(dp_index ^ near, core),
+            sources(dp_index ^ near, 1 - core),
+            sources(dp_index ^ far, 1 - core),
+            sources(dp_index ^ far, core),
+            sources(dp_index ^ 3, core),
+            sources(dp_index ^ 3, 1 - core),
+        ]
+    )
+    served = jnp.repeat(ordered % host_count == host_place, tokens)
+    ids = jnp.arange(3 * expert_total, dtype=jnp.int32) % expert_total
+    coded = arrived[:, 2 * width : 2 * width + 3 * expert_total].astype(jnp.float32)
+    prob = jnp.sum(jnp.where((ids == hosted)[None, :] & served[:, None], coded, 0.0), axis=1)
+    rows = jnp.where((prob != 0)[:, None], arrived[:, :width], jnp.zeros((), bf16))
+    gradient = (prob[:, None] * arrived[:, width : 2 * width].astype(jnp.float32)).astype(bf16)
+    back, incoming, outgoing = expert_rows(
+        rows, gradient, frozen_gate[0], frozen_up[0], frozen_down[0], owned_input, own_out
+    )
+    block_rows = 2 * half
+    own_back = back[:block_rows]
+    side_back = back[block_rows : 2 * block_rows]
+    cross_back = back[2 * block_rows : 3 * block_rows]
+    far_back = back[3 * block_rows :]
+
+    far_sum = add_rounded(far_back[:half], flip_core(far_back[half:], expert_count))
+    far_got = flip_plane(far_sum, dp_count, expert_count, (2, 1))
+    side_sum = side_back.astype(jnp.float32) + flip_core(cross_back, expert_count).astype(
+        jnp.float32
+    )
+    late = (side_sum[:half] + far_got.astype(jnp.float32)).astype(bf16)
+    early = side_sum[half:].astype(bf16)
+    early_got = flip_plane(early, dp_count, expert_count, (1, 2))
+    late_got = flip_plane(late, dp_count, expert_count, (1, 2))
+    mine_sum = own_back[:half].astype(jnp.float32) + late_got.astype(jnp.float32)
+    other_sum = add_rounded(own_back[half:], early_got)
+    mine_sum = mine_sum + flip_core(other_sum, expert_count).astype(jnp.float32)
+    pieces = mine_sum.reshape(chips, tokens, width)
+    total = pieces[0]
+    for z in range(1, chips):
+        total = total + flip_chip(pieces[z].astype(bf16), z, expert_count).astype(jnp.float32)
+    input_grad = total.astype(bf16)
+
+    slot_grad = jnp.concatenate([incoming, outgoing], axis=1).astype(bf16)
+    shares = lax.all_to_all(
+        slot_grad.reshape(dp_count, rank // dp_count, hidden + width),
+        "dp",
+        split_axis=0,
+        concat_axis=0,
+        tiled=True,
+    ).astype(jnp.float32)
+    summed = jnp.stack(
+        [
+            jnp.sum(jnp.where((local_of == which)[:, None, None], shares, 0.0), axis=0)
+            for which in range(local_experts)
+        ]
+    )
+    step_in, momentum_in, variance_in = adamw(
+        adapter_in, summed[:, :, :hidden], moment_in, second_in
+    )
+    step_out, momentum_out, variance_out = adamw(
+        adapter_out, summed[:, :, hidden:], moment_out, second_out
+    )
+    steps = jnp.concatenate([step_in, step_out], axis=2).astype(bf16)
+    copied = lax.all_to_all(
+        pick_local(steps, local_of), "dp", split_axis=0, concat_axis=0, tiled=True
+    ).reshape(1, rank, hidden + width)
+    return (
+        input_grad,
+        step_in,
+        step_out,
+        momentum_in,
+        momentum_out,
+        variance_in,
+        variance_out,
+        copied[:, :, :hidden],
+        copied[:, :, hidden:],
+    )
+
+
+def per_device(saved_input, output_grad, route_probs, expert_choice, *rest):
+    dp_count = lax.axis_size("dp")
+    expert_count = lax.axis_size("expert")
+    tokens, top_count = expert_choice.shape
+    local_experts = rest[4].shape[0]
+    devices = dp_count * expert_count
+    capacity = max(2, -(-3 * tokens * top_count // (2 * local_experts * expert_count)))
+    whole = dp_count == 4 and expert_count >= 4 and expert_count & (expert_count - 1) == 0
+    if whole and tokens <= 2 * capacity:
+        return dense_device(saved_input, output_grad, route_probs, expert_choice, *rest)
+    return packed_device(saved_input, output_grad, route_probs, expert_choice, *rest)
+
+
 def solution(mesh):
     return jax.shard_map(
         per_device,

time: 376 us -> 202 us (0.54)
  blocking collectives: 109 us -> 0 us
  waiting for transfers between devices: 125 us -> 70.2 us
  between operations: 15.1 us -> 2.2 us
  local copies, waits for them, and re-layouts: 37.7 us -> 28.2 us
  starting transfers between devices: 25.2 us -> 34.6 us
  matrix products: 33.9 us -> 42.3 us
  other arithmetic: 29.3 us -> 24 us
    all_to_all x5 -> x3, waiting for transfers between devices: 91.5 us -> 0.23 us  [the longest x1 0.22 us: dense_device(): lax.all_to_all(slot_grad.reshape(dp_count, rank // dp_count, hidden + wid...]
    ppermute x0 -> x17, waiting for transfers between devices: none -> 69.9 us  [the longest x5 45.4 us: flip_plane(): return lax.ppermute(array, ('dp', 'expert'), pairs)]
    all_gather x4 -> x0, blocking collectives: 68.7 us -> none  [the longest x1 37.8 us: per_device(): lax.all_gather(adapter_in.astype(jnp.bfloat16), 'dp', axis=1, tiled=True)]
    all_to_all x1 -> x0, blocking collectives: 39.9 us -> none  [per_device(): lax.all_to_all(picked_input, 'dp', split_axis=0, concat_axis=0, tiled=True)]
    reduce_scatter x2 -> x0, waiting for transfers between devices: 33.7 us -> none  [the longest x1 20 us: per_device(): lax.psum_scatter(placed_out, 'dp', scatter_dimension=1, tiled=True)]
    gather x5 -> x0, local copies, waits for them, and re-layouts: 25 us -> none  [the longest x1 6.43 us: pack_rows(): send_grad = jnp.take(scaled, filler, axis=0, mode='fill', fill_value=0)]
    ppermute x0 -> x17, starting transfers between devices: none -> 23.4 us  [the longest x6 13.2 us: flip_chip(): lax.ppermute(array, 'expert', [(i, i ^ 2 * distance) for i in range(size)])]
    all_to_all x5 -> x3, starting transfers between devices: 25.2 us -> 11.2 us  [the longest x1 4.06 us: dense_device(): lax.all_to_all(slot_grad.reshape(dp_count, rank // dp_count, hidden + wid...]
  transfers between devices with their start and end apart: 7 -> 20, of which waited for: 5 -> 11; matrix products, arithmetic and copies ran while one was open for 11% -> 22% of each run, Pallas kernels for 0% -> 0%
where the time goes in v1:
time: 202 us; the launch traced here: 201 us
  waiting for transfers between devices  70.2 us (35%)
  matrix products  42.3 us (21%)
  starting transfers between devices  34.6 us (17%)
  local copies, waits for them, and re-layouts  28.2 us (14%)
  other arithmetic  24 us (12%)
  between operations  2.2 us (1%)
    ppermute x5, waiting for transfers between devices, flip_plane(): return lax.ppermute(array, ('dp', 'expert'), pairs)  45.4 us
    dot_general x6, matrix products, contract_product(): lax.dot_general(left, right, (((left_dim,), (right_dim,)), ((), ())), pre...  32.7 us
    ppermute x6, waiting for transfers between devices, flip_chip(): lax.ppermute(array, 'expert', [(i, i ^ 2 * distance) for i in range(size)])  24.4 us
    unnamed x33, local copies, waits for them, and re-layouts  16.1 us
    ppermute x6, starting transfers between devices, flip_chip(): lax.ppermute(array, 'expert', [(i, i ^ 2 * distance) for i in range(size)])  13.2 us
    ppermute x5, starting transfers between devices, flip_plane(): return lax.ppermute(array, ('dp', 'expert'), pairs)  9.57 us
    another operation x5, other arithmetic  6.5 us
    dot_general x1, matrix products, expert_rows(): up_pre = jnp.dot(rows, up_weight, preferred_element_type=jnp.float32)  5.43 us
  transfers between devices with their start and end apart: 20, of which 11 were waited for; matrix products, arithmetic and copies ran while one was open for 22% of the time, Pallas kernels for 0%

profile of v1, /device:TPU:0, one launch (start us, length us, event | category | flops | bytes accessed | tf_op | source)
XLA Modules:
  0.0 201.4 jit_solution(16817335255373386481)
XLA Ops:
  2.9 3.1 %collective-permute-start = (bf16[32,4224]{1,0:T(8,128)(2,1)S(1)}, bf16[32,4224]{1,0:T(8,128)(2,1)S(1)}, u32[]{:S(2)}, u32[]{:S(2)}) collective-permute-start(bf16[32,4224]{1,0:T(8,128)(2,1)S(1)} %concatenate.35), channel_id=1, source_target_pairs={{0,2},{1,3},{2,0},{3,1},{4,6},{5,7},{6,4},{7,5},{8,10},{9,11},{10,... | collective-permute-start | bytes 811016 | tf_op jit(solution)/shard_map/ppermute | solution.py:194
  6.0 2.6 %collective-permute-start.1 = (bf16[32,4224]{1,0:T(8,128)(2,1)S(1)}, bf16[32,4224]{1,0:T(8,128)(2,1)S(1)}, u32[]{:S(2)}, u32[]{:S(2)}) collective-permute-start(bf16[32,4224]{1,0:T(8,128)(2,1)S(1)} %concatenate.35), channel_id=1, source_target_pairs={{0,4},{1,5},{2,6},{3,7},{4,0},{5,1},{6,2},{7,3},{8,12},{9,13},{10,... | collective-permute-start | bytes 811016 | tf_op jit(solution)/shard_map/ppermute | solution.py:194
  9.4 8.1 %collective-permute-done = bf16[32,4224]{1,0:T(8,128)(2,1)S(1)} collective-permute-done((bf16[32,4224]{1,0:T(8,128)(2,1)S(1)}, bf16[32,4224]{1,0:T(8,128)(2,1)S(1)}, u32[]{:S(2)}, u32[]{:S(2)}) %collective-permute-start) | collective-permute-done | bytes 270368 | tf_op jit(solution)/shard_map/ppermute | solution.py:194
  17.5 10.3 %collective-permute-done.1 = bf16[32,4224]{1,0:T(8,128)(2,1)S(1)} collective-permute-done((bf16[32,4224]{1,0:T(8,128)(2,1)S(1)}, bf16[32,4224]{1,0:T(8,128)(2,1)S(1)}, u32[]{:S(2)}, u32[]{:S(2)}) %collective-permute-start.1) | collective-permute-done | bytes 270368 | tf_op jit(solution)/shard_map/ppermute | solution.py:194
  36.1 23.2 %collective-permute-done.4 = bf16[256,4224]{1,0:T(8,128)(2,1)} collective-permute-done((bf16[256,4224]{1,0:T(8,128)(2,1)}, bf16[256,4224]{1,0:T(8,128)(2,1)}, u32[]{:S(2)}, u32[]{:S(2)}) %collective-permute-start.4) | collective-permute-done | bytes 2162720 | tf_op jit(solution)/shard_map/ppermute | solution.py:207
  60.2 3.7 %all-to-all-start = ((bf16[4,16,2816]{2,1,0:T(8,128)(2,1)}), bf16[4,16,2816]{2,1,0:T(8,128)(2,1)S(1)}, u32[]{:S(2)}, u32[]{:S(2)}) async-start(bf16[4,16,2816]{2,1,0:T(8,128)(2,1)} %select_select_fusion.1), calls=%async_computation | async-start | bytes 720896 | tf_op jit(solution)/shard_map/all_to_all | solution.py:312
  64.6 2.3 %slice.118 = bf16[128,4224]{1,0:T(8,128)(2,1)} slice(bf16[256,4224]{1,0:T(8,128)(2,1)} %collective-permute-done.4), slice={[0:128], [0:4224]} | slice | bytes 2162688 | tf_op jit(solution)/shard_map/slice | solution.py:324
  66.9 2.0 %collective-permute-start.6 = (bf16[128,4224]{1,0:T(8,128)(2,1)}, bf16[128,4224]{1,0:T(8,128)(2,1)}, u32[]{:S(2)}, u32[]{:S(2)}) collective-permute-start(bf16[128,4224]{1,0:T(8,128)(2,1)} %slice.118), channel_id=1, source_target_pairs={{0,16},{1,9},{2,18},{3,11},{4,20},{5,13},{6,22},{7,15},{8,24},{9,1... | collective-permute-start | bytes 3244040 | tf_op jit(solution)/shard_map/ppermute | solution.py:207
  73.2 3.1 %constant_dynamic-update-slice_fusion.8 = bf16[1024,4224]{1,0:T(8,128)(2,1)} fusion(bf16[1024,4224]{1,0:T(8,128)(2,1)} %get-tuple-element.28, bf16[256,4224]{1,0:T(8,128)(2,1)} %collective-permute-done.4), kind=kLoop, calls=%fused_computation.81 | loop fusion | bytes 4325376
  76.3 6.2 %collective-permute-done.6 = bf16[128,4224]{1,0:T(8,128)(2,1)} collective-permute-done((bf16[128,4224]{1,0:T(8,128)(2,1)}, bf16[128,4224]{1,0:T(8,128)(2,1)}, u32[]{:S(2)}, u32[]{:S(2)}) %collective-permute-start.6) | collective-permute-done | bytes 1081376 | tf_op jit(solution)/shard_map/ppermute | solution.py:207
  82.6 3.1 %constant_dynamic-update-slice_fusion.7 = bf16[1024,4224]{1,0:T(8,128)(2,1)} fusion(bf16[1024,4224]{1,0:T(8,128)(2,1)} %constant_dynamic-update-slice_fusion.8, bf16[256,4224]{1,0:T(8,128)(2,1)} %collective-permute-done.5), kind=kLoop, calls=%fused_computation.80 | loop fusion | bytes 4325376
  85.7 2.3 %constant_dynamic-update-slice_fusion.6 = bf16[1024,4224]{1,0:T(8,128)(2,1)} fusion(bf16[1024,4224]{1,0:T(8,128)(2,1)} %constant_dynamic-update-slice_fusion.7, bf16[128,4224]{1,0:T(8,128)(2,1)} %collective-permute-done.6), kind=kLoop, calls=%fused_computation.79 | loop fusion | bytes 2162688
  90.4 3.8 %convolution_convert_fusion.1 = bf16[1024,64]{0,1:T(8,128)(2,1)S(1)} fusion(bf16[64,2816]{1,0:T(8,128)(2,1)S(1)} %bitcast.42, bf16[1024,4224]{1,0:T(8,128)(2,1)} %constant_dynamic-update-slice_fusion.5, f32[1024]{0:T(1024)S(1)} %select_reduce_fusion), kind=kOutput, calls=%fused_computation.24 | convolution fusion | flops 274792448 | bytes 4591616 | tf_op jit(solution)/shard_map/dot_general | solution.py:17
  96.4 3.5 %fusion.2 = f32[1024,768]{1,0:T(8,128)S(1)} fusion(bf16[1,2048,768]{2,1,0:T(8,128)(2,1)S(1)} %copy-done.12, bf16[1024,4224]{1,0:T(8,128)(2,1)S(1)} %copy-done.9, pred[1024]{0:T(1024)(128)(4,1)S(1)} %broadcast_compare_fusion), kind=kOutput, calls=%fused_computation.5 | convolution fusion | flops 3223322624 | bytes 10486784 | tf_op jit(solution)/shard_map/dot_general | solution.py:249
  99.9 5.4 %multiply_convert_fusion.1 = (bf16[1024,768]{1,0:T(8,128)(2,1)S(1)}, f32[1024,768]{1,0:T(8,128)}) fusion(f32[1024,768]{1,0:T(8,128)S(1)} %fusion.2, bf16[1,2048,768]{2,1,0:T(8,128)(2,1)S(1)} %copy-done, bf16[1024,4224]{1,0:T(8,128)(2,1)S(1)} %copy-done.9, pred[1024]{0:T(1024)(128)(4,1)S(1)} %broadcast_compare_fusion), kind=kOutput, calls=%fused_computation.12 | convolution fusion | flops 3228041216 | bytes 15205376 | tf_op jit(solution)/shard_map/dot_general | solution.py:250
  105.3 5.2 %multiply_add_fusion = f32[1024,768]{1,0:T(8,128)} fusion(f32[1024,768]{1,0:T(8,128)S(1)} %fusion.32, bf16[1,768,2048]{2,1,0:T(8,128)(2,1)S(1)} %copy-done.11, bf16[1024,4224]{1,0:T(8,128)(2,1)S(1)} %copy-done.9, f32[1024]{0:T(1024)S(1)} %select_reduce_fusion), kind=kOutput, calls=%fused_computation.16 | convolution fusion | flops 3229089792 | bytes 13635584 | tf_op jit(solution)/shard_map/dot_general | solution.py:17
  110.5 10.4 %fusion = f32[1024,2048]{1,0:T(8,128)} fusion(bf16[1,2048,768]{2,1,0:T(8,128)(2,1)S(1)} %copy-done.12, f32[1024,768]{1,0:T(8,128)S(1)} %fusion.2, f32[1024,768]{1,0:T(8,128)} %multiply_add_fusion, f32[1024,768]{1,0:T(8,128)} %get-tuple-element.49), kind=kOutput, calls=%fused_computation.3 | convolution fusion | flops 3229089792 | bytes 20971520 | tf_op jit(solution)/shard_map/dot_general | solution.py:17
  120.9 7.0 %add_convert_fusion = bf16[1024,2048]{1,0:T(8,128)(2,1)S(1)} fusion(f32[1024,2048]{1,0:T(8,128)} %fusion, bf16[1,2048,768]{2,1,0:T(8,128)(2,1)S(1)} %copy-done, f32[1024,768]{1,0:T(8,128)} %multiply_add_fusion, f32[1024,768]{1,0:T(8,128)S(1)} %fusion.2), kind=kOutput, calls=%fused_computation | convolution fusion | flops 3230138368 | bytes 22020096 | tf_op jit(solution)/shard_map/dot_general | solution.py:17
  132.6 5.3 %fusion.9 = bf16[64,2048]{1,0:T(8,128)(2,1)} fusion(bf16[1024,768]{1,0:T(8,128)(2,1)} %copy-done.4, bf16[64,2816]{1,0:T(8,128)(2,1)S(1)} %bitcast.44, bf16[1024,4224]{1,0:T(8,128)(2,1)} %constant_dynamic-update-slice_fusion.5, f32[1024]{0:T(1024)S(1)} %select_reduce_fusion), kind=kOutput, calls=%fused_computation.18 | convolution fusion | flops 375717888 | bytes 6131712 | tf_op jit(solution)/shard_map/dot_general | solution.py:17
  139.6 4.1 %all-to-all-start.1 = ((bf16[4,16,2816]{2,1,0:T(8,128)(2,1)}), bf16[4,16,2816]{2,1,0:T(8,128)(2,1)S(1)}, u32[]{:S(2)}, u32[]{:S(2)}) async-start(bf16[4,16,2816]{2,1,0:T(8,128)(2,1)} %pad_maximum_fusion.1), calls=%async_computation.1 | async-start | bytes 720896 | tf_op jit(solution)/shard_map/all_to_all | solution.py:382
  147.8 2.0 %collective-permute-start.12 = (bf16[128,2048]{1,0:T(8,128)(2,1)}, bf16[128,2048]{1,0:T(8,128)(2,1)}, u32[]{:S(2)}, u32[]{:S(2)}) collective-permute-start(bf16[128,2048]{1,0:T(8,128)(2,1)} %slice.188), channel_id=1, source_target_pairs={{0,8},{1,17},{2,10},{3,19},{4,12},{5,21},{6,14},{7,23},{8,0},{9,25... | collective-permute-start | bytes 1572872 | tf_op jit(solution)/shard_map/ppermute | solution.py:207
  150.3 2.2 %fusion.44 = (bf16[2,16,2048]{2,1,0:T(8,128)(2,1)S(1)}, f32[2,16,2048]{2,1,0:T(8,128)}, f32[2,16,2048]{2,1,0:T(8,128)}, f32[2,16,2048]{2,1,0:T(8,128)}) fusion(f32[2,16,2048]{2,1,0:T(8,128)} %param.23, f32[1,16,2816]{2,1,0:T(8,128)S(1)} %bitcast.38, f32[1,16,2816]{2,1,0:T(8,128)S(1)} %bitcast.36, f32[2,16,2048]{2,1,0:T(8,128)} %param.25, ...), kind=kLoop, calls=%fused_computation.118 | loop fusion | flops 983040 | bytes 2064384 | tf_op jit(solution)/shard_map/convert.1
  152.6 4.7 %collective-permute-done.12 = bf16[128,2048]{1,0:T(8,128)(2,1)} collective-permute-done((bf16[128,2048]{1,0:T(8,128)(2,1)}, bf16[128,2048]{1,0:T(8,128)(2,1)}, u32[]{:S(2)}, u32[]{:S(2)}) %collective-permute-start.12) | collective-permute-done | bytes 524320 | tf_op jit(solution)/shard_map/ppermute | solution.py:207
  157.3 2.7 %add_convert_fusion.2 = (bf16[128,2048]{1,0:T(8,128)(2,1)S(1)}, bf16[128,2048]{1,0:T(8,128)(2,1)}) fusion(bf16[128,2048]{1,0:T(8,128)(2,1)} %collective-permute-done.9, bf16[1024,2048]{1,0:T(8,128)(2,1)} %copy-done.3, bf16[128,2048]{1,0:T(8,128)(2,1)} %collective-permute-done.12), kind=kLoop, calls=%fused_computation.32 | loop fusion | flops 2097152 | bytes 3145728 | tf_op jit(solution)/shard_map/convert_element_type | solution.py:211
  160.0 2.0 %collective-permute-start.10 = (bf16[128,2048]{1,0:T(8,128)(2,1)S(1)}, bf16[128,2048]{1,0:T(8,128)(2,1)S(1)}, u32[]{:S(2)}, u32[]{:S(2)}) collective-permute-start(bf16[128,2048]{1,0:T(8,128)(2,1)S(1)} %get-tuple-element.25), channel_id=1, source_target_pairs={{0,16},{1,9},{2,18},{3,11},{4,20},{5,13},{6,22},{7,15},{8,24},{9,1... | collective-permute-start | bytes 1572872 | tf_op jit(solution)/shard_map/ppermute | solution.py:207
  162.9 6.3 %collective-permute-done.10 = bf16[128,2048]{1,0:T(8,128)(2,1)S(1)} collective-permute-done((bf16[128,2048]{1,0:T(8,128)(2,1)S(1)}, bf16[128,2048]{1,0:T(8,128)(2,1)S(1)}, u32[]{:S(2)}, u32[]{:S(2)}) %collective-permute-start.10) | collective-permute-done | bytes 524320 | tf_op jit(solution)/shard_map/ppermute | solution.py:207
  170.1 2.0 %collective-permute-start.11 = (bf16[128,2048]{1,0:T(8,128)(2,1)}, bf16[128,2048]{1,0:T(8,128)(2,1)}, u32[]{:S(2)}, u32[]{:S(2)}) collective-permute-start(bf16[128,2048]{1,0:T(8,128)(2,1)} %fusion.15), channel_id=1, source_target_pairs={{0,8},{1,17},{2,10},{3,19},{4,12},{5,21},{6,14},{7,23},{8,0},{9,25... | collective-permute-start | bytes 1572872 | tf_op jit(solution)/shard_map/ppermute | solution.py:207
  173.0 3.5 %all-to-all-start.2 = ((bf16[4,16,2816]{2,1,0:T(8,128)(2,1)}), bf16[4,16,2816]{2,1,0:T(8,128)(2,1)S(1)}, u32[]{:S(2)}, u32[]{:S(2)}) async-start(bf16[4,16,2816]{2,1,0:T(8,128)(2,1)} %select_select_fusion), calls=%async_computation.2 | async-start | bytes 720896 | tf_op jit(solution)/shard_map/all_to_all | solution.py:402
  176.5 4.9 %collective-permute-done.11 = bf16[128,2048]{1,0:T(8,128)(2,1)} collective-permute-done((bf16[128,2048]{1,0:T(8,128)(2,1)}, bf16[128,2048]{1,0:T(8,128)(2,1)}, u32[]{:S(2)}, u32[]{:S(2)}) %collective-permute-start.11) | collective-permute-done | bytes 524320 | tf_op jit(solution)/shard_map/ppermute | solution.py:207
  181.4 2.6 %fusion.46 = (bf16[128,2048]{1,0:T(8,128)(2,1)S(1)}, f32[128,2048]{1,0:T(8,128)}) fusion(bf16[128,2048]{1,0:T(8,128)(2,1)} %collective-permute-done.13, bf16[128,2048]{1,0:T(8,128)(2,1)} %collective-permute-done.11, bf16[1024,2048]{1,0:T(8,128)(2,1)} %copy-done.3), kind=kLoop, calls=%fused_computation.119 | loop fusion | flops 1572864 | bytes 3145728 | tf_op jit(solution)/shard_map/convert.8
  184.8 5.0 %collective-permute-start.14 = (bf16[32,2048]{1,0:T(8,128)(2,1)}, bf16[32,2048]{1,0:T(8,128)(2,1)}, u32[]{:S(2)}, u32[]{:S(2)}) collective-permute-start(bf16[32,2048]{1,0:T(8,128)(2,1)} %get-tuple-element.29), channel_id=1, source_target_pairs={{0,2},{1,3},{2,0},{3,1},{4,6},{5,7},{6,4},{7,5},{8,10},{9,11},{10,... | collective-permute-start | bytes 393224 | tf_op jit(solution)/shard_map/ppermute | solution.py:194
  194.5 5.1 %collective-permute-done.15 = bf16[32,2048]{1,0:T(8,128)(2,1)} collective-permute-done((bf16[32,2048]{1,0:T(8,128)(2,1)}, bf16[32,2048]{1,0:T(8,128)(2,1)}, u32[]{:S(2)}, u32[]{:S(2)}) %collective-permute-start.15) | collective-permute-done | bytes 131104 | tf_op jit(solution)/shard_map/ppermute | solution.py:194
  (97 shorter events, 41.3 us)
Async XLA Ops:
  0.6 99.2 %copy-start = (bf16[1,2048,768]{2,1,0:T(8,128)(2,1)S(1)}, bf16[1,2048,768]{2,1,0:T(8,128)(2,1)}, u32[]{:S(2)}) copy-start(bf16[1,2048,768]{2,1,0:T(8,128)(2,1)} %param.20) | copy-start | bytes 9437188
  2.9 14.6 %collective-permute-start = (bf16[32,4224]{1,0:T(8,128)(2,1)S(1)}, bf16[32,4224]{1,0:T(8,128)(2,1)S(1)}, u32[]{:S(2)}, u32[]{:S(2)}) collective-permute-start(bf16[32,4224]{1,0:T(8,128)(2,1)S(1)} %concatenate.35), channel_id=1, source_target_pairs={{0,2},{1,3},{2,0},{3,1},{4,6},{5,7},{6,4},{7,5},{8,10},{9,11},{10,... | collective-permute-start | bytes 811016 | tf_op jit(solution)/shard_map/ppermute | solution.py:194
  6.0 21.8 %collective-permute-start.1 = (bf16[32,4224]{1,0:T(8,128)(2,1)S(1)}, bf16[32,4224]{1,0:T(8,128)(2,1)S(1)}, u32[]{:S(2)}, u32[]{:S(2)}) collective-permute-start(bf16[32,4224]{1,0:T(8,128)(2,1)S(1)} %concatenate.35), channel_id=1, source_target_pairs={{0,4},{1,5},{2,6},{3,7},{4,0},{5,1},{6,2},{7,3},{8,12},{9,13},{10,... | collective-permute-start | bytes 811016 | tf_op jit(solution)/shard_map/ppermute | solution.py:194
  8.6 19.3 %collective-permute-start.2 = (bf16[32,4224]{1,0:T(8,128)(2,1)S(1)}, bf16[32,4224]{1,0:T(8,128)(2,1)S(1)}, u32[]{:S(2)}, u32[]{:S(2)}) collective-permute-start(bf16[32,4224]{1,0:T(8,128)(2,1)S(1)} %concatenate.35), channel_id=1, source_target_pairs={{0,6},{1,7},{2,4},{3,5},{4,2},{5,3},{6,0},{7,1},{8,14},{9,15},{10,... | collective-permute-start | bytes 811016 | tf_op jit(solution)/shard_map/ppermute | solution.py:194
  27.9 5.8 %copy-start.5 = (f32[2,16,2048]{2,1,0:T(8,128)S(1)}, f32[2,16,2048]{2,1,0:T(8,128)}, u32[]{:S(2)}) copy-start(f32[2,16,2048]{2,1,0:T(8,128)} %param.23) | copy-start | bytes 786436
  27.9 6.7 %copy-start.10 = (s32[4,8]{1,0:T(4,128)S(1)}, s32[4,8]{1,0:T(4,128)}, u32[]{:S(2)}) copy-start(s32[4,8]{1,0:T(4,128)} %param.18) | copy-start | bytes 388
  27.9 2.8 %collective-permute-start.3 = (bf16[128,4224]{1,0:T(8,128)(2,1)S(1)}, bf16[128,4224]{1,0:T(8,128)(2,1)S(1)}, u32[]{:S(2)}, u32[]{:S(2)}) collective-permute-start(bf16[128,4224]{1,0:T(8,128)(2,1)S(1)} %pad_maximum_fusion), channel_id=1, source_target_pairs={{0,1},{1,0},{2,3},{3,2},{4,5},{5,4},{6,7},{7,6},{8,9},{9,8},{10,11... | collective-permute-start | bytes 3244040 | tf_op jit(solution)/shard_map/ppermute | solution.py:198
  32.2 27.1 %collective-permute-start.4 = (bf16[256,4224]{1,0:T(8,128)(2,1)}, bf16[256,4224]{1,0:T(8,128)(2,1)}, u32[]{:S(2)}, u32[]{:S(2)}) collective-permute-start(bf16[256,4224]{1,0:T(8,128)(2,1)} %get-tuple-element.27), channel_id=1, source_target_pairs={{0,8},{1,17},{2,10},{3,19},{4,12},{5,21},{6,14},{7,23},{8,0},{9,25... | collective-permute-start | bytes 6488072 | tf_op jit(solution)/shard_map/ppermute | solution.py:207
  59.3 23.3 %collective-permute-start.5 = (bf16[256,4224]{1,0:T(8,128)(2,1)}, bf16[256,4224]{1,0:T(8,128)(2,1)}, u32[]{:S(2)}, u32[]{:S(2)}) collective-permute-start(bf16[256,4224]{1,0:T(8,128)(2,1)} %collective-permute-done.4), channel_id=1, source_target_pairs={{0,1},{1,0},{2,3},{3,2},{4,5},{5,4},{6,7},{7,6},{8,9},{9,8},{10,11... | collective-permute-start | bytes 6488072 | tf_op jit(solution)/shard_map/ppermute | solution.py:198
  60.2 30.3 %all-to-all-start = ((bf16[4,16,2816]{2,1,0:T(8,128)(2,1)}), bf16[4,16,2816]{2,1,0:T(8,128)(2,1)S(1)}, u32[]{:S(2)}, u32[]{:S(2)}) async-start(bf16[4,16,2816]{2,1,0:T(8,128)(2,1)} %select_select_fusion.1), calls=%async_computation | async-start | bytes 720896 | tf_op jit(solution)/shard_map/all_to_all | solution.py:312
  66.9 15.6 %collective-permute-start.6 = (bf16[128,4224]{1,0:T(8,128)(2,1)}, bf16[128,4224]{1,0:T(8,128)(2,1)}, u32[]{:S(2)}, u32[]{:S(2)}) collective-permute-start(bf16[128,4224]{1,0:T(8,128)(2,1)} %slice.118), channel_id=1, source_target_pairs={{0,16},{1,9},{2,18},{3,11},{4,20},{5,13},{6,22},{7,15},{8,24},{9,1... | collective-permute-start | bytes 3244040 | tf_op jit(solution)/shard_map/ppermute | solution.py:207
  82.5 5.6 %collective-permute-start.7 = (bf16[128,4224]{1,0:T(8,128)(2,1)}, bf16[128,4224]{1,0:T(8,128)(2,1)S(1)}, u32[]{:S(2)}, u32[]{:S(2)}) collective-permute-start(bf16[128,4224]{1,0:T(8,128)(2,1)} %collective-permute-done.6), channel_id=1, source_target_pairs={{0,1},{1,0},{2,3},{3,2},{4,5},{5,4},{6,7},{7,6},{8,9},{9,8},{10,11... | collective-permute-start | bytes 3244040 | tf_op jit(solution)/shard_map/ppermute | solution.py:198
  90.4 4.7 %copy-start.9 = (bf16[1024,4224]{1,0:T(8,128)(2,1)S(1)}, bf16[1024,4224]{1,0:T(8,128)(2,1)}, u32[]{:S(2)}) copy-start(bf16[1024,4224]{1,0:T(8,128)(2,1)} %constant_dynamic-update-slice_fusion.5) | copy-start | bytes 25952260
  94.2 2.1 %copy-start.12 = (bf16[1,2048,768]{2,1,0:T(8,128)(2,1)S(1)}, bf16[1,2048,768]{2,1,0:T(8,128)(2,1)}, u32[]{:S(2)}) copy-start(bf16[1,2048,768]{2,1,0:T(8,128)(2,1)} %param.19) | copy-start | bytes 9437188
  99.9 5.4 %copy-start.11 = (bf16[1,768,2048]{2,1,0:T(8,128)(2,1)S(1)}, bf16[1,768,2048]{2,1,0:T(8,128)(2,1)}, u32[]{:S(2)}) copy-start(bf16[1,768,2048]{2,1,0:T(8,128)(2,1)} %param.21) | copy-start | bytes 9437188
  105.3 26.3 %copy-start.4 = (bf16[1024,768]{1,0:T(8,128)(2,1)}, bf16[1024,768]{1,0:T(8,128)(2,1)S(1)}, u32[]{:S(2)}) copy-start(bf16[1024,768]{1,0:T(8,128)(2,1)S(1)} %get-tuple-element.48) | copy-start | bytes 4718596
  128.0 2.4 %copy-start.3 = (bf16[1024,2048]{1,0:T(8,128)(2,1)}, bf16[1024,2048]{1,0:T(8,128)(2,1)S(1)}, u32[]{:S(2)}) copy-start(bf16[1024,2048]{1,0:T(8,128)(2,1)S(1)} %add_convert_fusion) | copy-start | bytes 12582916
  131.2 12.5 %collective-permute-start.8 = (bf16[256,2048]{1,0:T(8,128)(2,1)}, bf16[256,2048]{1,0:T(8,128)(2,1)}, u32[]{:S(2)}, u32[]{:S(2)}) collective-permute-start(bf16[256,2048]{1,0:T(8,128)(2,1)} %slice.128), channel_id=1, source_target_pairs={{0,1},{1,0},{2,3},{3,2},{4,5},{5,4},{6,7},{7,6},{8,9},{9,8},{10,11... | collective-permute-start | bytes 3145736 | tf_op jit(solution)/shard_map/ppermute | solution.py:198
  139.6 10.4 %all-to-all-start.1 = ((bf16[4,16,2816]{2,1,0:T(8,128)(2,1)}), bf16[4,16,2816]{2,1,0:T(8,128)(2,1)S(1)}, u32[]{:S(2)}, u32[]{:S(2)}) async-start(bf16[4,16,2816]{2,1,0:T(8,128)(2,1)} %pad_maximum_fusion.1), calls=%async_computation.1 | async-start | bytes 720896 | tf_op jit(solution)/shard_map/all_to_all | solution.py:382
  143.7 8.9 %collective-permute-start.9 = (bf16[128,2048]{1,0:T(8,128)(2,1)}, bf16[128,2048]{1,0:T(8,128)(2,1)}, u32[]{:S(2)}, u32[]{:S(2)}) collective-permute-start(bf16[128,2048]{1,0:T(8,128)(2,1)} %slice.131), channel_id=1, source_target_pairs={{0,1},{1,0},{2,3},{3,2},{4,5},{5,4},{6,7},{7,6},{8,9},{9,8},{10,11... | collective-permute-start | bytes 1572872 | tf_op jit(solution)/shard_map/ppermute | solution.py:198
  147.8 9.5 %collective-permute-start.12 = (bf16[128,2048]{1,0:T(8,128)(2,1)}, bf16[128,2048]{1,0:T(8,128)(2,1)}, u32[]{:S(2)}, u32[]{:S(2)}) collective-permute-start(bf16[128,2048]{1,0:T(8,128)(2,1)} %slice.188), channel_id=1, source_target_pairs={{0,8},{1,17},{2,10},{3,19},{4,12},{5,21},{6,14},{7,23},{8,0},{9,25... | collective-permute-start | bytes 1572872 | tf_op jit(solution)/shard_map/ppermute | solution.py:207
  150.1 11.9 %copy-start.6 = (f32[2,16,768]{2,1,0:T(8,128)S(1)}, f32[2,16,768]{2,1,0:T(8,128)}, u32[]{:S(2)}) copy-start(f32[2,16,768]{2,1,0:T(8,128)} %param.22) | copy-start | bytes 294916
  150.1 11.9 %copy-start.7 = (f32[2,16,768]{2,1,0:T(8,128)S(1)}, f32[2,16,768]{2,1,0:T(8,128)}, u32[]{:S(2)}) copy-start(f32[2,16,768]{2,1,0:T(8,128)} %param.24) | copy-start | bytes 294916
  150.1 11.9 %copy-start.8 = (f32[2,16,768]{2,1,0:T(8,128)S(1)}, f32[2,16,768]{2,1,0:T(8,128)}, u32[]{:S(2)}) copy-start(f32[2,16,768]{2,1,0:T(8,128)} %param.26) | copy-start | bytes 294916
  150.3 18.9 %copy-start.2 = (f32[256,2048]{1,0:T(8,128)S(1)}, f32[256,2048]{1,0:T(8,128)}, u32[]{:S(2)}) copy-start(f32[256,2048]{1,0:T(8,128)} %copy-done.1) | copy-start | bytes 6291460
  160.0 9.2 %collective-permute-start.10 = (bf16[128,2048]{1,0:T(8,128)(2,1)S(1)}, bf16[128,2048]{1,0:T(8,128)(2,1)S(1)}, u32[]{:S(2)}, u32[]{:S(2)}) collective-permute-start(bf16[128,2048]{1,0:T(8,128)(2,1)S(1)} %get-tuple-element.25), channel_id=1, source_target_pairs={{0,16},{1,9},{2,18},{3,11},{4,20},{5,13},{6,22},{7,15},{8,24},{9,1... | collective-permute-start | bytes 1572872 | tf_op jit(solution)/shard_map/ppermute | solution.py:207
  162.8 13.7 %collective-permute-start.13 = (bf16[128,2048]{1,0:T(8,128)(2,1)}, bf16[128,2048]{1,0:T(8,128)(2,1)}, u32[]{:S(2)}, u32[]{:S(2)}) collective-permute-start(bf16[128,2048]{1,0:T(8,128)(2,1)} %get-tuple-element.26), channel_id=1, source_target_pairs={{0,1},{1,0},{2,3},{3,2},{4,5},{5,4},{6,7},{7,6},{8,9},{9,8},{10,11... | collective-permute-start | bytes 1572872 | tf_op jit(solution)/shard_map/ppermute | solution.py:198
  170.1 11.3 %collective-permute-start.11 = (bf16[128,2048]{1,0:T(8,128)(2,1)}, bf16[128,2048]{1,0:T(8,128)(2,1)}, u32[]{:S(2)}, u32[]{:S(2)}) collective-permute-start(bf16[128,2048]{1,0:T(8,128)(2,1)} %fusion.15), channel_id=1, source_target_pairs={{0,8},{1,17},{2,10},{3,19},{4,12},{5,21},{6,14},{7,23},{8,0},{9,25... | collective-permute-start | bytes 1572872 | tf_op jit(solution)/shard_map/ppermute | solution.py:207
  173.0 19.2 %all-to-all-start.2 = ((bf16[4,16,2816]{2,1,0:T(8,128)(2,1)}), bf16[4,16,2816]{2,1,0:T(8,128)(2,1)S(1)}, u32[]{:S(2)}, u32[]{:S(2)}) async-start(bf16[4,16,2816]{2,1,0:T(8,128)(2,1)} %select_select_fusion), calls=%async_computation.2 | async-start | bytes 720896 | tf_op jit(solution)/shard_map/all_to_all | solution.py:402
  184.8 9.7 %collective-permute-start.14 = (bf16[32,2048]{1,0:T(8,128)(2,1)}, bf16[32,2048]{1,0:T(8,128)(2,1)}, u32[]{:S(2)}, u32[]{:S(2)}) collective-permute-start(bf16[32,2048]{1,0:T(8,128)(2,1)} %get-tuple-element.29), channel_id=1, source_target_pairs={{0,2},{1,3},{2,0},{3,1},{4,6},{5,7},{6,4},{7,5},{8,10},{9,11},{10,... | collective-permute-start | bytes 393224 | tf_op jit(solution)/shard_map/ppermute | solution.py:194
  189.7 9.8 %collective-permute-start.15 = (bf16[32,2048]{1,0:T(8,128)(2,1)}, bf16[32,2048]{1,0:T(8,128)(2,1)}, u32[]{:S(2)}, u32[]{:S(2)}) collective-permute-start(bf16[32,2048]{1,0:T(8,128)(2,1)} %get-tuple-element.31), channel_id=1, source_target_pairs={{0,4},{1,5},{2,6},{3,7},{4,0},{5,1},{6,2},{7,3},{8,12},{9,13},{10,... | collective-permute-start | bytes 393224 | tf_op jit(solution)/shard_map/ppermute | solution.py:194
  190.7 8.8 %collective-permute-start.16 = (bf16[32,2048]{1,0:T(8,128)(2,1)}, bf16[32,2048]{1,0:T(8,128)(2,1)}, u32[]{:S(2)}, u32[]{:S(2)}) collective-permute-start(bf16[32,2048]{1,0:T(8,128)(2,1)} %get-tuple-element.30), channel_id=1, source_target_pairs={{0,6},{1,7},{2,4},{3,5},{4,2},{5,3},{6,0},{7,1},{8,14},{9,15},{10,... | collective-permute-start | bytes 393224 | tf_op jit(solution)/shard_map/ppermute | solution.py:194
  (1 other events, 1.4 us)

commit v2 on v0

--- a/solution.py
+++ b/solution.py
@@ -1,6 +1,10 @@
+import functools
+
 import jax
 import jax.numpy as jnp
 from jax import lax
+from jax.experimental import pallas as pl
+from jax.experimental.pallas import tpu as pltpu
 from jax.sharding import PartitionSpec as P
 
 STEP = 100
@@ -11,6 +15,7 @@
 beta_two = 0.999
 decay_rate = 0.01
 adam_eps = 1e-08
+VMEM_LIMIT = 32 * 1024 * 1024
 
 
 def contract_product(left, right, left_dim, right_dim):
@@ -54,7 +59,7 @@
     return (step_dir, first_new, second_new)
 
 
-def per_device(
+def packed_device(
     saved_input,
     output_grad,
     route_probs,
@@ -82,7 +87,7 @@
     buffer_size = dp_count * expert_count * capacity
     source = dp_index * expert_count + column_index
     choice_flat = expert_choice.reshape(row_count)
-    dest_row, column, rank = route_rows(choice_flat, slot_expert, source, local_experts)
+    _, column, rank = route_rows(choice_flat, slot_expert, source, local_experts)
     scaled = (
         (route_probs[:, :, None] * output_grad[:, None, :].astype(jnp.float32))
         .astype(jnp.bfloat16)
@@ -190,6 +195,348 @@
     )
 
 
+def flip_chip(array, distance, size):
+    return lax.ppermute(array, "expert", [(i, i ^ (2 * distance)) for i in range(size)])
+
+
+def flip_core(array, size):
+    return lax.ppermute(array, "expert", [(i, i ^ 1) for i in range(size)])
+
+
+def flip_plane(array, dp_count, size, masks):
+    pairs = [
+        (row * size + col, (row ^ masks[col % 2]) * size + col)
+        for row in range(dp_count)
+        for col in range(size)
+    ]
+    return lax.ppermute(array, ("dp", "expert"), pairs)
+
+
+def add_rounded(left, right):
+    return (left.astype(jnp.float32) + right.astype(jnp.float32)).astype(jnp.bfloat16)
+
+
+def dense_probs(route_probs, expert_choice, expert_total):
+    ids = jnp.arange(expert_total, dtype=jnp.int32)
+    named = expert_choice[:, :, None] == ids[None, None, :]
+    return jnp.sum(jnp.where(named, route_probs[:, :, None], 0.0), axis=1)
+
+
+def split_three(value):
+    high = lax.reduce_precision(value, 8, 7)
+    rest = value - high
+    middle = lax.reduce_precision(rest, 8, 7)
+    low = rest - middle
+    return [part.astype(jnp.bfloat16) for part in (high, middle, low)]
+
+
+def pick_local(stacked, local_of):
+    count = stacked.shape[0]
+    total = jnp.zeros((local_of.shape[0],) + stacked.shape[1:], stacked.dtype)
+    for which in range(count):
+        chosen = (local_of == which).reshape((-1,) + (1,) * (stacked.ndim - 1))
+        total = jnp.where(chosen, stacked[which][None], total)
+    return total
+
+
+def transposed_dot(left, right):
+    return lax.dot_general(
+        left, right, (((1,), (1,)), ((), ())), preferred_element_type=jnp.float32
+    )
+
+
+def expert_kernel(sizes, out_sizes, places, chip_ids, token_rows, expert_total, hosts, *refs):
+    count = len(sizes)
+    pieces, refs = refs[:count], refs[count:]
+    gate_w, up_w, down_w, pair = refs[:4]
+    backs, refs = refs[4 : 4 + len(out_sizes)], refs[4 + len(out_sizes) :]
+    grads, given, grad_rows, hidden_s, gate_g, up_g, served = refs
+    dp_index, column_index = lax.axis_index("dp"), lax.axis_index("expert")
+    core = lax.rem(column_index, 2)
+    hosted = hosts[dp_index, column_index]
+    host_count, host_place = jnp.int32(0), jnp.int32(0)
+    for row in range(hosts.shape[0]):
+        same = (hosts[row, column_index] == hosted).astype(jnp.int32)
+        host_count = host_count + same
+        host_place = host_place + jnp.where(row < dp_index, same, 0)
+    width, hidden = gate_w.shape
+    total = given.shape[0]
+    coded_width = pieces[0].shape[1] - 2 * width
+    column = lax.broadcasted_iota(jnp.int32, (token_rows, coded_width), 1)
+    chosen = (lax.rem(column, expert_total) == hosted) & (column < 3 * expert_total)
+    for i, (masks, other, chip_id) in enumerate(
+        (masks, other, chip_id) for masks, other in places for chip_id in chip_ids
+    ):
+        row = lax.bitwise_xor(dp_index, jnp.where(core == 0, masks[0], masks[1]))
+        source_col = lax.bitwise_xor(column_index, 2 * chip_id + other)
+        source = row * hosts.shape[1] + source_col
+        served[i] = (lax.rem(source, host_count) == host_place).astype(jnp.int32)
+    start = 0
+    for piece, size in zip(pieces, sizes):
+
+        def prepare(j, carry, piece=piece, start=start):
+            here = pl.ds(pl.multiple_of(j * token_rows, token_rows), token_rows)
+            there = pl.ds(pl.multiple_of(start + j * token_rows, token_rows), token_rows)
+            coded = piece[here, 2 * width :].astype(jnp.float32)
+            prob = jnp.sum(jnp.where(chosen, coded, 0.0), axis=1, keepdims=True)
+            prob = jnp.where(served[start // token_rows + j] != 0, prob, 0.0)
+            keep = jnp.where(prob != 0, 1.0, 0.0).astype(jnp.bfloat16)
+            given[there, :] = piece[here, :width] * keep
+            gradient = piece[here, width : 2 * width].astype(jnp.float32)
+            grad_rows[there, :] = (prob * gradient).astype(jnp.bfloat16)
+            return carry
+
+        lax.fori_loop(0, size // token_rows, prepare, 0)
+        start += size
+    low_grad = transposed_dot(grad_rows[...], pair[:, hidden:]).astype(jnp.bfloat16)
+    tile = 256 if hidden % 256 == 0 else hidden
+
+    def middle(t, low_in):
+        cols = pl.ds(pl.multiple_of(t * tile, tile), tile)
+        gate = jnp.dot(given[...], gate_w[:, cols], preferred_element_type=jnp.float32)
+        up = jnp.dot(given[...], up_w[:, cols], preferred_element_type=jnp.float32)
+        sigmoid = jax.nn.sigmoid(gate)
+        owned = pair[:, cols]
+        state = (gate * sigmoid * up).astype(jnp.bfloat16)
+        hidden_s[:, cols] = state
+        grad = transposed_dot(grad_rows[...], down_w[cols, :])
+        grad = grad + adapter_scale_factor * jnp.dot(
+            low_grad, owned, preferred_element_type=jnp.float32
+        )
+        up_g[:, cols] = (grad * gate * sigmoid).astype(jnp.bfloat16)
+        gate_g[:, cols] = (grad * up * sigmoid * (1.0 + gate * (1.0 - sigmoid))).astype(
+            jnp.bfloat16
+        )
+        return low_in + transposed_dot(state, owned)
+
+    low_in = lax.fori_loop(
+        0, hidden // tile, middle, jnp.zeros((total, pair.shape[0]), jnp.float32)
+    )
+    wide = 256 if width % 256 == 0 else width
+
+    def last(t, carry):
+        cols = pl.ds(pl.multiple_of(t * wide, wide), wide)
+        back = transposed_dot(gate_g[...], gate_w[cols, :]) + transposed_dot(
+            up_g[...], up_w[cols, :]
+        )
+        begin = 0
+        for out, size in zip(backs, out_sizes):
+            out[:, cols] = back[begin : begin + size].astype(jnp.bfloat16)
+            begin += size
+        return carry
+
+    lax.fori_loop(0, width // wide, last, 0)
+    grads[:, :hidden] = adapter_scale_factor * contract_product(low_grad, hidden_s[...], 0, 0)
+    grads[:, hidden:] = adapter_scale_factor * contract_product(
+        low_in.astype(jnp.bfloat16), grad_rows[...], 0, 0
+    )
+
+
+def run_rows(
+    pieces, out_sizes, places, chip_ids, hosts, weights, pair, token_rows, expert_total
+):
+    gate, up, down = weights
+    width, hidden = gate.shape
+    sizes = [piece.shape[0] for piece in pieces]
+    total = sum(sizes)
+    rank = pair.shape[0]
+    local = pl.BlockSpec(memory_space=pltpu.VMEM)
+    bf16 = jnp.bfloat16
+    out = pl.pallas_call(
+        functools.partial(
+            expert_kernel, sizes, out_sizes, places, chip_ids, token_rows, expert_total
+        ),
+        out_shape=[jax.ShapeDtypeStruct((size, width), bf16) for size in out_sizes]
+        + [jax.ShapeDtypeStruct((rank, hidden + width), jnp.float32)],
+        in_specs=[pl.BlockSpec(memory_space=pltpu.SMEM)] + [local] * (len(pieces) + 4),
+        out_specs=[local] * (len(out_sizes) + 1),
+        scratch_shapes=[
+            pltpu.VMEM((total, width), bf16),
+            pltpu.VMEM((total, width), bf16),
+            pltpu.VMEM((total, hidden), bf16),
+            pltpu.VMEM((total, hidden), bf16),
+            pltpu.VMEM((total, hidden), bf16),
+            pltpu.SMEM((total // token_rows,), jnp.int32),
+        ],
+        compiler_params=pltpu.CompilerParams(vmem_limit_bytes=VMEM_LIMIT),
+        cost_estimate=pl.CostEstimate(
+            flops=2 * total * (5 * width * hidden + 3 * rank * (width + hidden)),
+            bytes_accessed=6 * width * hidden + total * 6 * width,
+            transcendentals=total * hidden,
+        ),
+    )(hosts, *pieces, gate, up, down, pair)
+    return list(out[:-1]), out[-1]
+
+
+def z_groups(chips):
+    return [[0, 1], list(range(2, chips))]
+
+
+def dense_device(
+    saved_input,
+    output_grad,
+    route_probs,
+    expert_choice,
+    slot_expert,
+    frozen_gate,
+    frozen_up,
+    frozen_down,
+    adapter_in,
+    adapter_out,
+    moment_in,
+    moment_out,
+    second_in,
+    second_out,
+):
+    dp_count = lax.axis_size("dp")
+    expert_count = lax.axis_size("expert")
+    column_index = lax.axis_index("expert")
+    local_experts = adapter_in.shape[0]
+    tokens, _ = expert_choice.shape
+    width = saved_input.shape[1]
+    hidden = adapter_in.shape[2]
+    expert_total = local_experts * expert_count
+    chips = expert_count // 2
+    bf16, f32 = jnp.bfloat16, jnp.float32
+    first, second = (1, 2), (2, 1)
+
+    parts = split_three(dense_probs(route_probs, expert_choice, expert_total))
+    spare = -(-3 * expert_total // 128) * 128 - 3 * expert_total
+    block = jnp.concatenate(
+        [saved_input, output_grad, *parts, jnp.zeros((tokens, spare), bf16)], axis=1
+    )
+    gathered = [block]
+    for z in range(1, chips):
+        gathered.append(flip_chip(block, z, expert_count))
+
+    hosts = lax.dynamic_index_in_dim(slot_expert, column_index, 1, keepdims=False)
+    local_of = hosts - local_experts * column_index
+    adapters = jnp.concatenate([adapter_in, adapter_out], axis=2).astype(bf16)
+    rank = dp_count * adapter_in.shape[1]
+    pair = lax.all_to_all(
+        pick_local(adapters, local_of), "dp", split_axis=0, concat_axis=0, tiled=True
+    ).reshape(rank, hidden + width)
+
+    weights = (frozen_gate[0], frozen_up[0], frozen_down[0])
+
+    def compute(pieces, out_sizes, places, chip_ids):
+        return run_rows(
+            pieces, out_sizes, places, chip_ids, slot_expert, weights, pair, tokens, expert_total
+        )
+
+    grads = []
+    returned = {}
+
+    def rows_of(pieces, out_sizes, places, chip_ids):
+        backs, grad = compute(pieces, out_sizes, places, chip_ids)
+        grads.append(grad)
+        return backs
+
+    own_places = [((0, 0), 0), ((0, 0), 1)]
+    side_places = [(first, 0), (first, 1)]
+    cross_places = [(second, 1), (second, 0)]
+    far_places = [((3, 3), 0), ((3, 3), 1)]
+    groups = z_groups(chips)
+    for number, chip_ids in enumerate(groups):
+        half = len(chip_ids) * tokens
+        mine = jnp.concatenate([gathered[z] for z in chip_ids], axis=0)
+        if number == 0:
+            mine, pair = lax.optimization_barrier((mine, pair))
+        other = flip_core(mine, expert_count)
+        own = jnp.concatenate([mine, other], axis=0)
+        side = flip_plane(own, dp_count, expert_count, first)
+        far_mine = flip_plane(side[:half], dp_count, expert_count, second)
+        cross = flip_core(side, expert_count)
+        far_other = flip_core(far_mine, expert_count)
+        if number + 1 < len(groups):
+            own_mine, own_other = rows_of([own], [half, half], own_places, chip_ids)
+            side_late, side_early, cross_back, far_back, far_away = rows_of(
+                [side, cross, far_mine, far_other],
+                [half, half, 2 * half, half, half],
+                side_places + cross_places + far_places,
+                chip_ids,
+            )
+        else:
+            own_mine, own_other, side_late, side_early = rows_of(
+                [own, side], [half] * 4, own_places + side_places, chip_ids
+            )
+            cross_back, far_back, far_away = rows_of(
+                [cross, far_mine, far_other],
+                [2 * half, half, half],
+                cross_places + far_places,
+                chip_ids,
+            )
+        far_got_core = flip_core(far_away, expert_count)
+        far_sum = add_rounded(far_back, far_got_core)
+        far_got = flip_plane(far_sum, dp_count, expert_count, second)
+        cross_got = flip_core(cross_back, expert_count)
+        early = add_rounded(side_early, cross_got[half:])
+        early_got = flip_plane(early, dp_count, expert_count, first)
+        other_sum = add_rounded(own_other, early_got)
+        other_got = flip_core(other_sum, expert_count)
+        late = (
+            side_late.astype(f32) + cross_got[:half].astype(f32) + far_got.astype(f32)
+        ).astype(bf16)
+        late_got = flip_plane(late, dp_count, expert_count, first)
+        total = (own_mine.astype(f32) + other_got.astype(f32) + late_got.astype(f32)).astype(bf16)
+        for i, z in enumerate(chip_ids):
+            piece = total[i * tokens : (i + 1) * tokens]
+            returned[z] = piece if z == 0 else flip_chip(piece, z, expert_count)
+    input_grad = sum(piece.astype(f32) for piece in returned.values()).astype(bf16)
+
+    slot_grad = sum(grads).astype(bf16)
+    shares = lax.all_to_all(
+        slot_grad.reshape(dp_count, rank // dp_count, hidden + width),
+        "dp",
+        split_axis=0,
+        concat_axis=0,
+        tiled=True,
+    ).astype(f32)
+    summed = jnp.stack(
+        [
+            jnp.sum(jnp.where((local_of == which)[:, None, None], shares, 0.0), axis=0)
+            for which in range(local_experts)
+        ]
+    )
+    step_in, momentum_in, variance_in = adamw(
+        adapter_in, summed[:, :, :hidden], moment_in, second_in
+    )
+    step_out, momentum_out, variance_out = adamw(
+        adapter_out, summed[:, :, hidden:], moment_out, second_out
+    )
+    steps = jnp.concatenate([step_in, step_out], axis=2).astype(bf16)
+    copied = lax.all_to_all(
+        pick_local(steps, local_of), "dp", split_axis=0, concat_axis=0, tiled=True
+    ).reshape(1, rank, hidden + width)
+    return (
+        input_grad,
+        step_in,
+        step_out,
+        momentum_in,
+        momentum_out,
+        variance_in,
+        variance_out,
+        copied[:, :, :hidden],
+        copied[:, :, hidden:],
+    )
+
+
+def runs_dense(dp_count, expert_count):
+    return dp_count == 4 and expert_count == 8
+
+
+def per_device(saved_input, output_grad, route_probs, expert_choice, *rest):
+    dp_count = lax.axis_size("dp")
+    expert_count = lax.axis_size("expert")
+    tokens, top_count = expert_choice.shape
+    local_experts = rest[4].shape[0]
+    row_count = tokens * top_count
+    capacity = max(2, -(-3 * row_count // (2 * local_experts * expert_count)))
+    if tokens <= 2 * capacity and runs_dense(dp_count, expert_count):
+        return dense_device(saved_input, output_grad, route_probs, expert_choice, *rest)
+    return packed_device(saved_input, output_grad, route_probs, expert_choice, *rest)
+
+
 def solution(mesh):
     return jax.shard_map(
         per_device,

time: 376 us -> 163 us (0.43)
  blocking collectives: 109 us -> 0 us
  waiting for transfers between devices: 125 us -> 63.7 us
  Pallas kernels: 0 us -> 36.9 us
  matrix products: 33.9 us -> 0 us
  local copies, waits for them, and re-layouts: 37.7 us -> 12.4 us
  other arithmetic: 29.3 us -> 14.1 us
  between operations: 15.1 us -> 1.09 us
  starting transfers between devices: 25.2 us -> 33.8 us
    all_to_all x5 -> x3, waiting for transfers between devices: 91.5 us -> 3.66 us  [the longest x1 3.65 us: dense_device(): lax.all_to_all(slot_grad.reshape(dp_count, rank // dp_count, hidden + wid...]
    all_gather x4 -> x0, blocking collectives: 68.7 us -> none  [the longest x1 37.8 us: per_device(): lax.all_gather(adapter_in.astype(jnp.bfloat16), 'dp', axis=1, tiled=True)]
    ppermute x0 -> x28, waiting for transfers between devices: none -> 60.1 us  [the longest x10 38.9 us: flip_plane(): return lax.ppermute(array, ('dp', 'expert'), pairs)]
    all_to_all x1 -> x0, blocking collectives: 39.9 us -> none  [per_device(): lax.all_to_all(picked_input, 'dp', split_axis=0, concat_axis=0, tiled=True)]
    pallas_call x0 -> x4, Pallas kernels: none -> 36.9 us  [run_rows(): pl.pallas_call(functools.partial(expert_kernel, sizes, out_sizes, places,...]
    dot_general x9 -> x0, matrix products: 33.9 us -> none  [the longest x6 23.4 us: contract_product(): lax.dot_general(left, right, (((left_dim,), (right_dim,)), ((), ())), pre...]
    reduce_scatter x2 -> x0, waiting for transfers between devices: 33.7 us -> none  [the longest x1 20 us: per_device(): lax.psum_scatter(placed_out, 'dp', scatter_dimension=1, tiled=True)]
    gather x5 -> x0, local copies, waits for them, and re-layouts: 25 us -> none  [the longest x1 6.43 us: pack_rows(): send_grad = jnp.take(scaled, filler, axis=0, mode='fill', fill_value=0)]
  transfers between devices with their start and end apart: 7 -> 31, of which waited for: 5 -> 9; matrix products, arithmetic and copies ran while one was open for 11% -> 11% of each run, Pallas kernels for 0% -> 23%
where the time goes in v2:
time: 163 us; the launch traced here: 162 us
  waiting for transfers between devices  63.7 us (39%)
  Pallas kernels  36.9 us (23%)
  starting transfers between devices  33.8 us (21%)
  other arithmetic  14.1 us (9%)
  local copies, waits for them, and re-layouts  12.4 us (8%)
    ppermute x10, waiting for transfers between devices, flip_plane(): return lax.ppermute(array, ('dp', 'expert'), pairs)  38.9 us
    pallas_call x4, Pallas kernels, run_rows(): pl.pallas_call(functools.partial(expert_kernel, sizes, out_sizes, places,...  36.9 us
    ppermute x6, waiting for transfers between devices, flip_chip(): lax.ppermute(array, 'expert', [(i, i ^ 2 * distance) for i in range(size)])  21.1 us
    ppermute x10, starting transfers between devices, flip_plane(): return lax.ppermute(array, ('dp', 'expert'), pairs)  11.7 us
    ppermute x6, starting transfers between devices, flip_chip(): lax.ppermute(array, 'expert', [(i, i ^ 2 * distance) for i in range(size)])  8.9 us
    unnamed x67, local copies, waits for them, and re-layouts  8.88 us
    all_to_all x1, starting transfers between devices, dense_device(): lax.all_to_all(pick_local(adapters, local_of), 'dp', split_axis=0, concat...  4.07 us
    all_to_all x1, waiting for transfers between devices, dense_device(): lax.all_to_all(slot_grad.reshape(dp_count, rank // dp_count, hidden + wid...  3.65 us
  transfers between devices with their start and end apart: 31, of which 9 were waited for; matrix products, arithmetic and copies ran while one was open for 11% of the time, Pallas kernels for 23%

profile of v2, /device:TPU:0, one launch (start us, length us, event | category | flops | bytes accessed | tf_op | source)
XLA Modules:
  0.0 162.0 jit_solution(15205277507901044458)
XLA Ops:
  1.6 1.8 %concatenate.24 = bf16[32,4224]{1,0:T(8,128)(2,1)} concatenate(bf16[32,2048]{1,0:T(8,128)(2,1)} %param.14, bf16[32,2048]{1,0:T(8,128)(2,1)} %param.15, bf16[32,16]{1,0:T(8,128)(2,1)S(1)} %get-tuple-element.73, bf16[32,16]{1,0:T(8,128)(2,1)S(1)} %get-tuple-element.72, bf16[32,16]{1,0:T(8,128)(2,1)S(1)} %get-tuple-element.71, bf16[32,80]{1,0:T(8,128)(2,1)S(1)} %broadcast_in_dim.86), dimensions={1} | concatenate | bytes 540672 | tf_op jit(solution)/shard_map/concatenate | solution.py:405
  3.3 5.1 %collective-permute-start.14 = (bf16[32,4224]{1,0:T(8,128)(2,1)}, bf16[32,4224]{1,0:T(8,128)(2,1)}, u32[]{:S(2)}, u32[]{:S(2)}) collective-permute-start(bf16[32,4224]{1,0:T(8,128)(2,1)} %concatenate.24), channel_id=1, source_target_pairs={{0,6},{1,7},{2,4},{3,5},{4,2},{5,3},{6,0},{7,1},{8,14},{9,15},{10,... | collective-permute-start | bytes 811016 | tf_op jit(solution)/shard_map/ppermute | solution.py:199
  11.9 4.1 %all-to-all-start = ((bf16[4,16,2816]{2,1,0:T(8,128)(2,1)}), bf16[4,16,2816]{2,1,0:T(8,128)(2,1)S(1)}, u32[]{:S(2)}, u32[]{:S(2)}) async-start(bf16[4,16,2816]{2,1,0:T(8,128)(2,1)} %select_select_fusion.1), calls=%async_computation | async-start | bytes 720896 | tf_op jit(solution)/shard_map/all_to_all | solution.py:416
  16.0 10.2 %collective-permute-done = bf16[32,4224]{1,0:T(8,128)(2,1)} collective-permute-done((bf16[32,4224]{1,0:T(8,128)(2,1)}, bf16[32,4224]{1,0:T(8,128)(2,1)}, u32[]{:S(2)}, u32[]{:S(2)}) %collective-permute-start) | collective-permute-done | bytes 270368 | tf_op jit(solution)/shard_map/ppermute | solution.py:199
  26.1 1.9 %pad_maximum_fusion = bf16[64,4224]{1,0:T(8,128)(2,1)} fusion(bf16[32,4224]{1,0:T(8,128)(2,1)} %collective-permute-done, bf16[32,4224]{1,0:T(8,128)(2,1)} %concatenate.24), kind=kLoop, calls=%fused_computation.5 | loop fusion | flops 1081344 | bytes 1081344 | tf_op jit(solution)/shard_map/concatenate | solution.py:442
  28.0 1.1 constant_dynamic-update-slice_fusion.1
  29.1 2.6 %collective-permute-done.13 = bf16[32,4224]{1,0:T(8,128)(2,1)} collective-permute-done((bf16[32,4224]{1,0:T(8,128)(2,1)}, bf16[32,4224]{1,0:T(8,128)(2,1)}, u32[]{:S(2)}, u32[]{:S(2)}) %collective-permute-start.13) | collective-permute-done | bytes 270368 | tf_op jit(solution)/shard_map/ppermute | solution.py:199
  31.7 1.2 pad_maximum_fusion.1
  34.0 1.0 constant_dynamic-update-slice_fusion.3
  35.1 1.6 collective-permute-start.2
  37.3 13.0 %collective-permute-done.2.refs_0_ = bf16[128,4224]{1,0:T(8,128)(2,1)S(1)} collective-permute-done((bf16[128,4224]{1,0:T(8,128)(2,1)S(1)}, bf16[128,4224]{1,0:T(8,128)(2,1)S(1)}, u32[]{:S(2)}, u32[]{:S(2)}) %collective-permute-start.2) | collective-permute-done | bytes 1081376 | tf_op jit(solution)/shard_map/ppermute | solution.py:212
  50.3 1.6 collective-permute-start.4
  51.9 15.7 %collective-permute-done.16.refs_1_ = bf16[128,4224]{1,0:T(8,128)(2,1)S(1)} collective-permute-done((bf16[128,4224]{1,0:T(8,128)(2,1)S(1)}, bf16[128,4224]{1,0:T(8,128)(2,1)S(1)}, u32[]{:S(2)}, u32[]{:S(2)}) %collective-permute-start.16) | collective-permute-done | bytes 1081376 | tf_op jit(solution)/shard_map/ppermute | solution.py:212
  67.7 1.6 collective-permute-start.18
  69.8 7.1 %shard_map.205 = (bf16[64,2048]{1,0:T(8,128)(2,1)S(1)}, bf16[64,2048]{1,0:T(8,128)(2,1)S(1)}, f32[64,2816]{1,0:T(8,128)S(1)}) custom-call(s32[4,8]{1,0:T(4,128)S(1)} %copy-done.23, bf16[128,4224]{1,0:T(8,128)(2,1)S(1)} %constant_dynamic-update-slice_fusion.refs_0_, bf16[2048,768]{1,0:T(8,128)(2,1)S(1)} %bitcast.16, bf16[2048,768]{1,0:T(8,128)(2,1)S(1)} %bitcast.20, ...), custom_call_target="tpu_custom_call" | custom-call | flops 2151677952 | bytes 11010048 | tf_op jit(solution)/shard_map/pallas_call | solution.py:345
  78.3 8.9 %shard_map.207 = (bf16[64,2048]{1,0:T(8,128)(2,1)S(1)}, bf16[64,2048]{1,0:T(8,128)(2,1)S(1)}, bf16[64,2048]{1,0:T(8,128)(2,1)S(1)}, bf16[64,2048]{1,0:T(8,128)(2,1)S(1)}, f32[64,2816]{1,0:T(8,128)S(1)}) custom-call(s32[4,8]{1,0:T(4,128)S(1)} %copy-done.23, bf16[128,4224]{1,0:T(8,128)(2,1)S(1)} %constant_dynamic-update-slice_fusion.2.refs_0_, ...), custom_call_target="tpu_custom_call" | custom-call | flops 4303355904 | bytes 12582912 | tf_op jit(solution)/shard_map/pallas_call | solution.py:345
  90.0 12.1 %shard_map.206 = (bf16[64,2048]{1,0:T(8,128)(2,1)S(1)}, bf16[64,2048]{1,0:T(8,128)(2,1)S(1)}, bf16[128,2048]{1,0:T(8,128)(2,1)}, bf16[64,2048]{1,0:T(8,128)(2,1)...) custom-call(s32[4,8]{1,0:T(4,128)S(1)} %copy-done.23, bf16[128,4224]{1,0:T(8,128)(2,1)S(1)} %collective-permute-done.2.refs_0_, ...), custom_call_target="tpu_custom_call" | custom-call | flops 6455033856 | bytes 14155776 | tf_op jit(solution)/shard_map/pallas_call | solution.py:345
  104.0 8.9 %shard_map.208 = (bf16[128,2048]{1,0:T(8,128)(2,1)S(1)}, bf16[64,2048]{1,0:T(8,128)(2,1)S(1)}, bf16[64,2048]{1,0:T(8,128)(2,1)S(1)}, f32[64,2816]{1,0:T(8,128)S(1)}) custom-call(s32[4,8]{1,0:T(4,128)S(1)} %copy-done.23, bf16[128,4224]{1,0:T(8,128)(2,1)S(1)} %collective-permute-done.17.refs_0_, bf16[64,4224]{1,0:T(8,128)(2,1)S(1)} %collective-permute-done.18.refs_1_, ...), custom_call_target="tpu_custom_call" | custom-call | flops 4303355904 | bytes 12582912 | tf_op jit(solution)/shard_map/pallas_call | solution.py:345
  114.0 3.6 %all-to-all-start.1 = ((bf16[4,16,2816]{2,1,0:T(8,128)(2,1)}), bf16[4,16,2816]{2,1,0:T(8,128)(2,1)S(1)}, u32[]{:S(2)}, u32[]{:S(2)}) async-start(bf16[4,16,2816]{2,1,0:T(8,128)(2,1)} %bitcast.6), calls=%async_computation.1 | async-start | bytes 720896 | tf_op jit(solution)/shard_map/all_to_all | solution.py:488
  118.2 1.1 add_convert_fusion.8
  119.3 1.9 %collective-permute-start.10 = (bf16[64,2048]{1,0:T(8,128)(2,1)S(1)}, bf16[64,2048]{1,0:T(8,128)(2,1)S(1)}, u32[]{:S(2)}, u32[]{:S(2)}) collective-permute-start(bf16[64,2048]{1,0:T(8,128)(2,1)S(1)} %add_convert_fusion.8), channel_id=1, source_target_pairs={{0,16},{1,9},{2,18},{3,11},{4,20},{5,13},{6,22},{7,15},{8,24},{9,1... | collective-permute-start | bytes 786440 | tf_op jit(solution)/shard_map/ppermute | solution.py:212
  121.5 3.7 %all-to-all-done.1 = bf16[4,16,2816]{2,1,0:T(8,128)(2,1)S(1)} async-done(((bf16[4,16,2816]{2,1,0:T(8,128)(2,1)}), bf16[4,16,2816]{2,1,0:T(8,128)(2,1)S(1)}, u32[]{:S(2)}, u32[]{:S(2)}) %all-to-all-start.1) | async-done | bytes 360480 | tf_op jit(solution)/shard_map/all_to_all | solution.py:488
  126.2 1.0 fusion.13
  128.1 3.5 %all-to-all-start.2 = ((bf16[4,16,2816]{2,1,0:T(8,128)(2,1)}), bf16[4,16,2816]{2,1,0:T(8,128)(2,1)S(1)}, u32[]{:S(2)}, u32[]{:S(2)}) async-start(bf16[4,16,2816]{2,1,0:T(8,128)(2,1)} %select_select_fusion), calls=%async_computation.2 | async-start | bytes 720896 | tf_op jit(solution)/shard_map/all_to_all | solution.py:508
  131.6 1.3 add_convert_fusion.10
  132.9 2.0 %collective-permute-start.7 = (bf16[64,2048]{1,0:T(8,128)(2,1)S(1)}, bf16[64,2048]{1,0:T(8,128)(2,1)S(1)}, u32[]{:S(2)}, u32[]{:S(2)}) collective-permute-start(bf16[64,2048]{1,0:T(8,128)(2,1)S(1)} %get-tuple-element.61), channel_id=1, source_target_pairs={{0,8},{1,17},{2,10},{3,19},{4,12},{5,21},{6,14},{7,23},{8,0},{9,25... | collective-permute-start | bytes 786440 | tf_op jit(solution)/shard_map/ppermute | solution.py:212
  135.2 2.0 %collective-permute-start.21 = (bf16[64,2048]{1,0:T(8,128)(2,1)S(1)}, bf16[64,2048]{1,0:T(8,128)(2,1)S(1)}, u32[]{:S(2)}, u32[]{:S(2)}) collective-permute-start(bf16[64,2048]{1,0:T(8,128)(2,1)S(1)} %get-tuple-element.63), channel_id=1, source_target_pairs={{0,8},{1,17},{2,10},{3,19},{4,12},{5,21},{6,14},{7,23},{8,0},{9,25... | collective-permute-start | bytes 786440 | tf_op jit(solution)/shard_map/ppermute | solution.py:212
  137.3 2.8 %collective-permute-done.7 = bf16[64,2048]{1,0:T(8,128)(2,1)S(1)} collective-permute-done((bf16[64,2048]{1,0:T(8,128)(2,1)S(1)}, bf16[64,2048]{1,0:T(8,128)(2,1)S(1)}, u32[]{:S(2)}, u32[]{:S(2)}) %collective-permute-start.7) | collective-permute-done | bytes 262176 | tf_op jit(solution)/shard_map/ppermute | solution.py:212
  140.4 5.4 %collective-permute-done.21 = bf16[64,2048]{1,0:T(8,128)(2,1)S(1)} collective-permute-done((bf16[64,2048]{1,0:T(8,128)(2,1)S(1)}, bf16[64,2048]{1,0:T(8,128)(2,1)S(1)}, u32[]{:S(2)}, u32[]{:S(2)}) %collective-permute-start.21) | collective-permute-done | bytes 262176 | tf_op jit(solution)/shard_map/ppermute | solution.py:212
  146.6 2.0 %collective-permute-done.25 = bf16[64,2048]{1,0:T(8,128)(2,1)S(1)} collective-permute-done((bf16[64,2048]{1,0:T(8,128)(2,1)S(1)}, bf16[64,2048]{1,0:T(8,128)(2,1)S(1)}, u32[]{:S(2)}, u32[]{:S(2)}) %collective-permute-start.25) | collective-permute-done | bytes 262176 | tf_op jit(solution)/shard_map/ppermute | solution.py:212
  149.4 2.1 %collective-permute-start.27 = (bf16[32,2048]{1,0:T(8,128)(2,1)S(1)}, bf16[32,2048]{1,0:T(8,128)(2,1)S(1)}, u32[]{:S(2)}, u32[]{:S(2)}) collective-permute-start(bf16[32,2048]{1,0:T(8,128)(2,1)S(1)} %get-tuple-element.66), channel_id=1, source_target_pairs={{0,6},{1,7},{2,4},{3,5},{4,2},{5,3},{6,0},{7,1},{8,14},{9,15},{10,... | collective-permute-start | bytes 393224 | tf_op jit(solution)/shard_map/ppermute | solution.py:199
  152.9 8.4 %collective-permute-done.26 = bf16[32,2048]{1,0:T(8,128)(2,1)S(1)} collective-permute-done((bf16[32,2048]{1,0:T(8,128)(2,1)S(1)}, bf16[32,2048]{1,0:T(8,128)(2,1)S(1)}, u32[]{:S(2)}, u32[]{:S(2)}) %collective-permute-start.26) | collective-permute-done | bytes 131104 | tf_op jit(solution)/shard_map/ppermute | solution.py:199
  (138 shorter events, 21.1 us)
Async XLA Ops:
  3.3 25.8 %collective-permute-start.14 = (bf16[32,4224]{1,0:T(8,128)(2,1)}, bf16[32,4224]{1,0:T(8,128)(2,1)}, u32[]{:S(2)}, u32[]{:S(2)}) collective-permute-start(bf16[32,4224]{1,0:T(8,128)(2,1)} %concatenate.24), channel_id=1, source_target_pairs={{0,6},{1,7},{2,4},{3,5},{4,2},{5,3},{6,0},{7,1},{8,14},{9,15},{10,... | collective-permute-start | bytes 811016 | tf_op jit(solution)/shard_map/ppermute | solution.py:199
  8.4 23.3 %collective-permute-start.13 = (bf16[32,4224]{1,0:T(8,128)(2,1)}, bf16[32,4224]{1,0:T(8,128)(2,1)}, u32[]{:S(2)}, u32[]{:S(2)}) collective-permute-start(bf16[32,4224]{1,0:T(8,128)(2,1)} %concatenate.24), channel_id=1, source_target_pairs={{0,4},{1,5},{2,6},{3,7},{4,0},{5,1},{6,2},{7,3},{8,12},{9,13},{10,... | collective-permute-start | bytes 811016 | tf_op jit(solution)/shard_map/ppermute | solution.py:199
  8.4 17.7 %collective-permute-start = (bf16[32,4224]{1,0:T(8,128)(2,1)}, bf16[32,4224]{1,0:T(8,128)(2,1)}, u32[]{:S(2)}, u32[]{:S(2)}) collective-permute-start(bf16[32,4224]{1,0:T(8,128)(2,1)} %concatenate.24), channel_id=1, source_target_pairs={{0,2},{1,3},{2,0},{3,1},{4,6},{5,7},{6,4},{7,5},{8,10},{9,11},{10,... | collective-permute-start | bytes 811016 | tf_op jit(solution)/shard_map/ppermute | solution.py:199
  11.1 58.7 %copy-start.2 = (bf16[1,768,2048]{2,1,0:T(8,128)(2,1)S(1)}, bf16[1,768,2048]{2,1,0:T(8,128)(2,1)}, u32[]{:S(2)}) copy-start(bf16[1,768,2048]{2,1,0:T(8,128)(2,1)} %param.21) | copy-start | bytes 9437188
  11.9 16.1 %all-to-all-start = ((bf16[4,16,2816]{2,1,0:T(8,128)(2,1)}), bf16[4,16,2816]{2,1,0:T(8,128)(2,1)S(1)}, u32[]{:S(2)}, u32[]{:S(2)}) async-start(bf16[4,16,2816]{2,1,0:T(8,128)(2,1)} %select_select_fusion.1), calls=%async_computation | async-start | bytes 720896 | tf_op jit(solution)/shard_map/all_to_all | solution.py:416
  28.0 7.0 %collective-permute-start.1 = (bf16[64,4224]{1,0:T(8,128)(2,1)}, bf16[64,4224]{1,0:T(8,128)(2,1)S(1)}, u32[]{:S(2)}, u32[]{:S(2)}) collective-permute-start(bf16[64,4224]{1,0:T(8,128)(2,1)} %pad_maximum_fusion), channel_id=1, source_target_pairs={{0,1},{1,0},{2,3},{3,2},{4,5},{5,4},{6,7},{7,6},{8,9},{9,8},{10,11... | collective-permute-start | bytes 1622024 | tf_op jit(solution)/shard_map/ppermute | solution.py:203
  33.0 3.7 %collective-permute-start.15 = (bf16[64,4224]{1,0:T(8,128)(2,1)S(1)}, bf16[64,4224]{1,0:T(8,128)(2,1)S(1)}, u32[]{:S(2)}, u32[]{:S(2)}) collective-permute-start(bf16[64,4224]{1,0:T(8,128)(2,1)S(1)} %pad_maximum_fusion.1), channel_id=1, source_target_pairs={{0,1},{1,0},{2,3},{3,2},{4,5},{5,4},{6,7},{7,6},{8,9},{9,8},{10,11... | collective-permute-start | bytes 1622024 | tf_op jit(solution)/shard_map/ppermute | solution.py:203
  35.1 15.2 %collective-permute-start.2 = (bf16[128,4224]{1,0:T(8,128)(2,1)S(1)}, bf16[128,4224]{1,0:T(8,128)(2,1)S(1)}, u32[]{:S(2)}, u32[]{:S(2)}) collective-permute-start(bf16[128,4224]{1,0:T(8,128)(2,1)S(1)} %constant_dynamic-update-slice_fusion.refs_0_), channel_id=1, source_target_pairs={{0,8},{1,17},{2,10},{3,19},{4,12},{5,21},{6,14},{7,23},{8,0},{9,25... | collective-permute-start | bytes 3244040 | tf_op jit(solution)/shard_map/ppermute | solution.py:212
  36.7 31.0 %collective-permute-start.16 = (bf16[128,4224]{1,0:T(8,128)(2,1)S(1)}, bf16[128,4224]{1,0:T(8,128)(2,1)S(1)}, u32[]{:S(2)}, u32[]{:S(2)}) collective-permute-start(bf16[128,4224]{1,0:T(8,128)(2,1)S(1)} %constant_dynamic-update-slice_fusion.2.refs_0_), channel_id=1, source_target_pairs={{0,8},{1,17},{2,10},{3,19},{4,12},{5,21},{6,14},{7,23},{8,0},{9,25... | collective-permute-start | bytes 3244040 | tf_op jit(solution)/shard_map/ppermute | solution.py:212
  50.3 19.0 %collective-permute-start.4 = (bf16[64,4224]{1,0:T(8,128)(2,1)S(1)}, bf16[64,4224]{1,0:T(8,128)(2,1)S(1)}, u32[]{:S(2)}, u32[]{:S(2)}) collective-permute-start(bf16[64,4224]{1,0:T(8,128)(2,1)S(1)} %slice.74), channel_id=1, source_target_pairs={{0,16},{1,9},{2,18},{3,11},{4,20},{5,13},{6,22},{7,15},{8,24},{9,1... | collective-permute-start | bytes 1622024 | tf_op jit(solution)/shard_map/ppermute | solution.py:212
  51.9 38.1 %collective-permute-start.3 = (bf16[128,4224]{1,0:T(8,128)(2,1)S(1)}, bf16[128,4224]{1,0:T(8,128)(2,1)S(1)}, u32[]{:S(2)}, u32[]{:S(2)}) collective-permute-start(bf16[128,4224]{1,0:T(8,128)(2,1)S(1)} %collective-permute-done.2.refs_0_), channel_id=1, source_target_pairs={{0,1},{1,0},{2,3},{3,2},{4,5},{5,4},{6,7},{7,6},{8,9},{9,8},{10,11... | collective-permute-start | bytes 3244040 | tf_op jit(solution)/shard_map/ppermute | solution.py:203
  67.7 22.2 %collective-permute-start.18 = (bf16[64,4224]{1,0:T(8,128)(2,1)S(1)}, bf16[64,4224]{1,0:T(8,128)(2,1)S(1)}, u32[]{:S(2)}, u32[]{:S(2)}) collective-permute-start(bf16[64,4224]{1,0:T(8,128)(2,1)S(1)} %slice.79), channel_id=1, source_target_pairs={{0,16},{1,9},{2,18},{3,11},{4,20},{5,13},{6,22},{7,15},{8,24},{9,1... | collective-permute-start | bytes 1622024 | tf_op jit(solution)/shard_map/ppermute | solution.py:212
  69.3 34.7 %collective-permute-start.17 = (bf16[128,4224]{1,0:T(8,128)(2,1)S(1)}, bf16[128,4224]{1,0:T(8,128)(2,1)S(1)}, u32[]{:S(2)}, u32[]{:S(2)}) collective-permute-start(bf16[128,4224]{1,0:T(8,128)(2,1)S(1)} %collective-permute-done.16.refs_1_), channel_id=1, source_target_pairs={{0,1},{1,0},{2,3},{3,2},{4,5},{5,4},{6,7},{7,6},{8,9},{9,8},{10,11... | collective-permute-start | bytes 3244040 | tf_op jit(solution)/shard_map/ppermute | solution.py:203
  69.3 20.7 %collective-permute-start.5 = (bf16[64,4224]{1,0:T(8,128)(2,1)S(1)}, bf16[64,4224]{1,0:T(8,128)(2,1)S(1)}, u32[]{:S(2)}, u32[]{:S(2)}) collective-permute-start(bf16[64,4224]{1,0:T(8,128)(2,1)S(1)} %collective-permute-done.4.refs_2_), channel_id=1, source_target_pairs={{0,1},{1,0},{2,3},{3,2},{4,5},{5,4},{6,7},{7,6},{8,9},{9,8},{10,11... | collective-permute-start | bytes 1622024 | tf_op jit(solution)/shard_map/ppermute | solution.py:203
  89.9 14.1 %collective-permute-start.19 = (bf16[64,4224]{1,0:T(8,128)(2,1)S(1)}, bf16[64,4224]{1,0:T(8,128)(2,1)S(1)}, u32[]{:S(2)}, u32[]{:S(2)}) collective-permute-start(bf16[64,4224]{1,0:T(8,128)(2,1)S(1)} %collective-permute-done.18.refs_1_), channel_id=1, source_target_pairs={{0,1},{1,0},{2,3},{3,2},{4,5},{5,4},{6,7},{7,6},{8,9},{9,8},{10,11... | collective-permute-start | bytes 1622024 | tf_op jit(solution)/shard_map/ppermute | solution.py:203
  103.5 14.7 %collective-permute-start.9 = (bf16[64,2048]{1,0:T(8,128)(2,1)}, bf16[64,2048]{1,0:T(8,128)(2,1)}, u32[]{:S(2)}, u32[]{:S(2)}) collective-permute-start(bf16[64,2048]{1,0:T(8,128)(2,1)} %get-tuple-element.37), channel_id=1, source_target_pairs={{0,1},{1,0},{2,3},{3,2},{4,5},{5,4},{6,7},{7,6},{8,9},{9,8},{10,11... | collective-permute-start | bytes 786440 | tf_op jit(solution)/shard_map/ppermute | solution.py:203
  104.0 27.6 %collective-permute-start.6 = (bf16[128,2048]{1,0:T(8,128)(2,1)}, bf16[128,2048]{1,0:T(8,128)(2,1)}, u32[]{:S(2)}, u32[]{:S(2)}) collective-permute-start(bf16[128,2048]{1,0:T(8,128)(2,1)} %get-tuple-element.34), channel_id=1, source_target_pairs={{0,1},{1,0},{2,3},{3,2},{4,5},{5,4},{6,7},{7,6},{8,9},{9,8},{10,11... | collective-permute-start | bytes 1572872 | tf_op jit(solution)/shard_map/ppermute | solution.py:203
  114.0 11.2 %all-to-all-start.1 = ((bf16[4,16,2816]{2,1,0:T(8,128)(2,1)}), bf16[4,16,2816]{2,1,0:T(8,128)(2,1)S(1)}, u32[]{:S(2)}, u32[]{:S(2)}) async-start(bf16[4,16,2816]{2,1,0:T(8,128)(2,1)} %bitcast.6), calls=%async_computation.1 | async-start | bytes 720896 | tf_op jit(solution)/shard_map/all_to_all | solution.py:488
  117.6 3.7 %collective-permute-start.23 = (bf16[64,2048]{1,0:T(8,128)(2,1)}, bf16[64,2048]{1,0:T(8,128)(2,1)S(1)}, u32[]{:S(2)}, u32[]{:S(2)}) collective-permute-start(bf16[64,2048]{1,0:T(8,128)(2,1)} %copy-done.25), channel_id=1, source_target_pairs={{0,1},{1,0},{2,3},{3,2},{4,5},{5,4},{6,7},{7,6},{8,9},{9,8},{10,11... | collective-permute-start | bytes 786440 | tf_op jit(solution)/shard_map/ppermute | solution.py:203
  118.1 16.9 %collective-permute-start.20 = (bf16[128,2048]{1,0:T(8,128)(2,1)}, bf16[128,2048]{1,0:T(8,128)(2,1)S(1)}, u32[]{:S(2)}, u32[]{:S(2)}) collective-permute-start(bf16[128,2048]{1,0:T(8,128)(2,1)} %copy-done.24), channel_id=1, source_target_pairs={{0,1},{1,0},{2,3},{3,2},{4,5},{5,4},{6,7},{7,6},{8,9},{9,8},{10,11... | collective-permute-start | bytes 1572872 | tf_op jit(solution)/shard_map/ppermute | solution.py:203
  119.3 12.3 %collective-permute-start.10 = (bf16[64,2048]{1,0:T(8,128)(2,1)S(1)}, bf16[64,2048]{1,0:T(8,128)(2,1)S(1)}, u32[]{:S(2)}, u32[]{:S(2)}) collective-permute-start(bf16[64,2048]{1,0:T(8,128)(2,1)S(1)} %add_convert_fusion.8), channel_id=1, source_target_pairs={{0,16},{1,9},{2,18},{3,11},{4,20},{5,13},{6,22},{7,15},{8,24},{9,1... | collective-permute-start | bytes 786440 | tf_op jit(solution)/shard_map/ppermute | solution.py:212
  121.3 13.7 %collective-permute-start.24 = (bf16[64,2048]{1,0:T(8,128)(2,1)S(1)}, bf16[64,2048]{1,0:T(8,128)(2,1)S(1)}, u32[]{:S(2)}, u32[]{:S(2)}) collective-permute-start(bf16[64,2048]{1,0:T(8,128)(2,1)S(1)} %add_convert_fusion.3), channel_id=1, source_target_pairs={{0,16},{1,9},{2,18},{3,11},{4,20},{5,13},{6,22},{7,15},{8,24},{9,1... | collective-permute-start | bytes 786440 | tf_op jit(solution)/shard_map/ppermute | solution.py:212
  128.1 23.4 %all-to-all-start.2 = ((bf16[4,16,2816]{2,1,0:T(8,128)(2,1)}), bf16[4,16,2816]{2,1,0:T(8,128)(2,1)S(1)}, u32[]{:S(2)}, u32[]{:S(2)}) async-start(bf16[4,16,2816]{2,1,0:T(8,128)(2,1)} %select_select_fusion), calls=%async_computation.2 | async-start | bytes 720896 | tf_op jit(solution)/shard_map/all_to_all | solution.py:508
  132.9 7.3 %collective-permute-start.7 = (bf16[64,2048]{1,0:T(8,128)(2,1)S(1)}, bf16[64,2048]{1,0:T(8,128)(2,1)S(1)}, u32[]{:S(2)}, u32[]{:S(2)}) collective-permute-start(bf16[64,2048]{1,0:T(8,128)(2,1)S(1)} %get-tuple-element.61), channel_id=1, source_target_pairs={{0,8},{1,17},{2,10},{3,19},{4,12},{5,21},{6,14},{7,23},{8,0},{9,25... | collective-permute-start | bytes 786440 | tf_op jit(solution)/shard_map/ppermute | solution.py:212
  134.9 11.1 %collective-permute-start.11 = (bf16[64,2048]{1,0:T(8,128)(2,1)S(1)}, bf16[64,2048]{1,0:T(8,128)(2,1)S(1)}, u32[]{:S(2)}, u32[]{:S(2)}) collective-permute-start(bf16[64,2048]{1,0:T(8,128)(2,1)S(1)} %get-tuple-element.62), channel_id=1, source_target_pairs={{0,8},{1,17},{2,10},{3,19},{4,12},{5,21},{6,14},{7,23},{8,0},{9,25... | collective-permute-start | bytes 786440 | tf_op jit(solution)/shard_map/ppermute | solution.py:212
  135.2 10.5 %collective-permute-start.21 = (bf16[64,2048]{1,0:T(8,128)(2,1)S(1)}, bf16[64,2048]{1,0:T(8,128)(2,1)S(1)}, u32[]{:S(2)}, u32[]{:S(2)}) collective-permute-start(bf16[64,2048]{1,0:T(8,128)(2,1)S(1)} %get-tuple-element.63), channel_id=1, source_target_pairs={{0,8},{1,17},{2,10},{3,19},{4,12},{5,21},{6,14},{7,23},{8,0},{9,25... | collective-permute-start | bytes 786440 | tf_op jit(solution)/shard_map/ppermute | solution.py:212
  137.2 11.3 %collective-permute-start.25 = (bf16[64,2048]{1,0:T(8,128)(2,1)S(1)}, bf16[64,2048]{1,0:T(8,128)(2,1)S(1)}, u32[]{:S(2)}, u32[]{:S(2)}) collective-permute-start(bf16[64,2048]{1,0:T(8,128)(2,1)S(1)} %get-tuple-element.64), channel_id=1, source_target_pairs={{0,8},{1,17},{2,10},{3,19},{4,12},{5,21},{6,14},{7,23},{8,0},{9,25... | collective-permute-start | bytes 786440 | tf_op jit(solution)/shard_map/ppermute | solution.py:212
  140.2 5.8 %collective-permute-start.8 = (bf16[64,2048]{1,0:T(8,128)(2,1)S(1)}, bf16[64,2048]{1,0:T(8,128)(2,1)S(1)}, u32[]{:S(2)}, u32[]{:S(2)}) collective-permute-start(bf16[64,2048]{1,0:T(8,128)(2,1)S(1)} %add_convert_fusion.9), channel_id=1, source_target_pairs={{0,1},{1,0},{2,3},{3,2},{4,5},{5,4},{6,7},{7,6},{8,9},{9,8},{10,11... | collective-permute-start | bytes 786440 | tf_op jit(solution)/shard_map/ppermute | solution.py:203
  145.8 2.7 %collective-permute-start.22 = (bf16[64,2048]{1,0:T(8,128)(2,1)S(1)}, bf16[64,2048]{1,0:T(8,128)(2,1)S(1)}, u32[]{:S(2)}, u32[]{:S(2)}) collective-permute-start(bf16[64,2048]{1,0:T(8,128)(2,1)S(1)} %add_convert_fusion.4), channel_id=1, source_target_pairs={{0,1},{1,0},{2,3},{3,2},{4,5},{5,4},{6,7},{7,6},{8,9},{9,8},{10,11... | collective-permute-start | bytes 786440 | tf_op jit(solution)/shard_map/ppermute | solution.py:203
  146.1 6.7 %collective-permute-start.12 = (bf16[32,2048]{1,0:T(8,128)(2,1)S(1)}, bf16[32,2048]{1,0:T(8,128)(2,1)S(1)}, u32[]{:S(2)}, u32[]{:S(2)}) collective-permute-start(bf16[32,2048]{1,0:T(8,128)(2,1)S(1)} %slice.78), channel_id=1, source_target_pairs={{0,2},{1,3},{2,0},{3,1},{4,6},{5,7},{6,4},{7,5},{8,10},{9,11},{10,... | collective-permute-start | bytes 393224 | tf_op jit(solution)/shard_map/ppermute | solution.py:199
  148.7 12.6 %collective-permute-start.26 = (bf16[32,2048]{1,0:T(8,128)(2,1)S(1)}, bf16[32,2048]{1,0:T(8,128)(2,1)S(1)}, u32[]{:S(2)}, u32[]{:S(2)}) collective-permute-start(bf16[32,2048]{1,0:T(8,128)(2,1)S(1)} %get-tuple-element.65), channel_id=1, source_target_pairs={{0,4},{1,5},{2,6},{3,7},{4,0},{5,1},{6,2},{7,3},{8,12},{9,13},{10,... | collective-permute-start | bytes 393224 | tf_op jit(solution)/shard_map/ppermute | solution.py:199
  149.4 11.8 %collective-permute-start.27 = (bf16[32,2048]{1,0:T(8,128)(2,1)S(1)}, bf16[32,2048]{1,0:T(8,128)(2,1)S(1)}, u32[]{:S(2)}, u32[]{:S(2)}) collective-permute-start(bf16[32,2048]{1,0:T(8,128)(2,1)S(1)} %get-tuple-element.66), channel_id=1, source_target_pairs={{0,6},{1,7},{2,4},{3,5},{4,2},{5,3},{6,0},{7,1},{8,14},{9,15},{10,... | collective-permute-start | bytes 393224 | tf_op jit(solution)/shard_map/ppermute | solution.py:199
  (31 other events, 201.5 us)
